TPU v7x, 128 devices: a whole 4x4x4 slice. The times are simulated.
128 devices in a mesh: seg: 16 (over z, y_lo, core), section: 8 (over y_hi, x).
Axes of the slice: x: 4, y: 4 (y_hi: 2, y_lo: 2; y = y_hi * 2 + y_lo), z: 4, core: 2. Of those that a mesh axis runs over, the one named last changes fastest.
Arguments:
- leaving: bfloat16 [16, 8, 272, 4096], P('seg', 'section'), may hold values from -6 to 6
- w_query: bfloat16 [8, 4096, 2048], P('section'), may hold values from -0.09375 to 0.09375
- w_key: bfloat16 [8, 4096, 2048], P('section', None, 'seg'), may hold values from -0.09375 to 0.09375
- w_value: bfloat16 [8, 4096, 4096], P('section', None, 'seg'), may hold values from -0.09375 to 0.09375
- w_gate: bfloat16 [8, 4096], P('section'), may hold values from -0.09375 to 0.09375
- norm_gain: bfloat16 [8, 4096], P('section'), may hold values from 0.5 to 1.5
- memory_matrix: bfloat16 [8, 4096, 2048], P('section', 'seg'), may hold values from -24 to 24
- key_totals: float32 [8, 2048], P('section'), may hold values from 0.02 to 0.5
- doc_starts: int32 [8, 16], P('section'), may hold values 0 or 1
Outputs:
- updated: bfloat16 [16, 8, 272, 4096], P('seg', 'section')
- matrix_next: bfloat16 [8, 4096, 2048], P('section', 'seg')
- totals_next: float32 [8, 2048], P('section')
All inputs are finite; a program needn't handle non-finite values. No bound on the sum of `doc_starts` on one device may be relied on, other than what follows from the above.
Results may differ from a plain program's by a relative error of at most 0.01.
Values may be sent and summed in bfloat16 or wider, within the bound.
No kernel may reach another device: no remote copies, remote signals or barrier semaphores. Data moves between devices by JAX's collectives and lax.ppermute only.
A program may use at most 128 MiB of HBM per device.

v0:
```python
import jax
import jax.numpy as jnp
from jax import lax
from jax.experimental import pallas as pl
from jax.experimental.pallas import tpu as pltpu
from jax.sharding import PartitionSpec as P


MEM = 16
EPS = 1e-05
INTERPRET = False
F32 = jnp.float32
BF16 = jnp.bfloat16


VM = pl.BlockSpec(memory_space=pltpu.VMEM)
SM = pl.BlockSpec(memory_space=pltpu.SMEM)


def permute(block, axis, target):
    size = lax.axis_size(axis)
    return lax.ppermute(block, axis, [(i, target(i)) for i in range(size)])


def shifted(block):
    return permute(block, "section", lambda i: (i + 1) % lax.axis_size("section"))


def shifted_across(block):
    wide = lax.axis_size("section")
    pairs = [
        (s * wide + p, (s ^ 2) * wide + (p + 1) % wide)
        for s in range(lax.axis_size("seg"))
        for p in range(wide)
    ]
    return lax.ppermute(block, ("seg", "section"), pairs)


def shifted_rows(block):
    wide, run = lax.axis_size("section"), lax.axis_size("section") // 2
    ends = [p for p in range(wide) if p % run == run - 1]
    segs = range(lax.axis_size("seg"))
    late = [s for s in segs if (s ^ (s // 2)) % 2]

    def send(part, pairs):
        return lax.ppermute(part, ("seg", "section"), [(s * wide + p, s * wide + q) for s, p, q in pairs])

    plain = send(block, [(s, p, p + 1) for s in segs for p in range(wide) if p not in ends])
    first = send(block, [(s, p, (p + 1) % wide) for s in segs if s not in late for p in ends])
    second = send(block, [(s, p, (p + run) % wide) for s in late for p in ends])
    second = send(second, [(s, p, p + 1 - run) for s in late for p in ends])
    source = jnp.where(
        lax.axis_index("section") % run > 0, 0,
        jnp.where(jnp.isin(lax.axis_index("seg"), jnp.array(late)), 2, 1),
    )
    return source.astype(jnp.int32)[None], plain, first, second


def offsets():
    return [(dz, dy, dc) for dc in (0, 1) for dy in (0, 1) for dz in (0, 3, 1, 2)]


def gather_slots(block):
    def send(part, target):
        return permute(part, "seg", target)

    below = send(block, lambda i: (i + 4) % 16)
    above = send(block, lambda i: (i - 4) % 16)
    far = send(block, lambda i: i ^ 8)
    near = jnp.stack([block, below, above, far])
    across = send(near, lambda i: i ^ 2)
    return near, across, send(near, lambda i: i ^ 1), send(across, lambda i: i ^ 1)


def gather_pairs(block):
    def send(part, target):
        return permute(part, "seg", target)

    below = send(block, lambda i: (i + 4) % 16)
    above = send(block, lambda i: (i - 4) % 16)
    far = send(block, lambda i: i ^ 8)
    mine = (block, below, above, far)
    return mine + tuple(send(part, lambda i: i ^ 1) for part in mine)


def pair_offsets():
    return [(dz, dy, dc) for dc in (0, 1) for dz in (0, 3, 1, 2) for dy in (0, 1)]


def slot_segments(me, order):
    z, y, c = me // 4, (me // 2) % 2, me % 2
    dz, dy, dc = (jnp.array(v, jnp.int32) for v in zip(*order))
    return ((z + dz) % 4) * 4 + (y ^ dy) * 2 + (c ^ dc)


def split(x):
    high = x.astype(BF16)
    return high, (x - high.astype(F32)).astype(BF16)


def dot(a, b, contract=((1,), (0,))):
    return lax.dot_general(a, b, (contract, ((), ())), preferred_element_type=F32)


def dot3(a, b):
    ah, al = a
    bh, bl = b
    return dot(ah, bh) + (dot(ah, bl) + dot(al, bh))


def phi(x):
    return jnp.where(x > 0, x, jnp.exp(jnp.minimum(x, 0.0)) - 1.0) + 1.0


def normalise(rows, gain):
    wide = rows.astype(F32)
    inverse = lax.rsqrt(jnp.mean(wide * wide, axis=-1, keepdims=True) + EPS)
    return (wide * inverse * gain.astype(F32)).astype(BF16)


def last_starts(starts_ref, count):
    lasts, last = [], jnp.int32(-1)
    for s in range(count):
        last = jnp.where(starts_ref[0, s] == 1, jnp.int32(s), last)
        lasts.append(last)
    return lasts


def norm_kernel(rows_ref, across_ref, gain_ref, out_ref):
    out_ref[0] = normalise(rows_ref[...], gain_ref[...])
    out_ref[1] = normalise(across_ref[...], gain_ref[...])


def kv_kernel(slots_ref, *refs):
    pairs, (key_ref, value_ref, gate_ref, key_out, value_out, gate_out) = refs[:8], refs[8:]
    count = 16
    memory = jnp.concatenate([ref[...] for ref in pairs], axis=0)
    memory = memory.reshape(count * MEM, memory.shape[2])
    keys = phi(dot(memory, key_ref[...])).astype(BF16)
    values = dot(memory, value_ref[...])
    gate = jnp.broadcast_to(gate_ref[...], (8, gate_ref.shape[1]))
    rates = jax.nn.sigmoid(dot(memory, gate, ((1,), (1,))))[:, :1]
    rates = jnp.broadcast_to(rates, (count * MEM, 128))
    for slot in range(count):
        rows = pl.ds(pl.multiple_of(slots_ref[slot] * MEM, MEM), MEM)
        part = slice(slot * MEM, (slot + 1) * MEM)
        key_out[rows, :] = keys[part]
        value_out[rows, :] = values[part]
        gate_out[rows, :] = rates[part]


def solve_kernel(slots_ref, starts_ref, a_ref, b_ref, c_ref, d_ref, values_ref, rates_ref, matrix_ref, totals_ref, keys_out, writes_out, sent_out):
    pieces = (a_ref, b_ref, c_ref, d_ref)
    each, rows, width = a_ref.shape
    count = 4 * each
    for slot in range(count):
        cols = pl.ds(pl.multiple_of(slots_ref[slot] * width, width), width)
        keys_out[:, cols] = pieces[slot // each][slot % each]
    keys = keys_out[...]
    gram = dot(keys, keys, ((1,), (1,)))
    probed = dot(keys, matrix_ref[...], ((1,), (1,)))
    own = lax.broadcasted_iota(jnp.int32, (rows, 1), 0) // MEM
    other = lax.broadcasted_iota(jnp.int32, (rows, rows), 1) // MEM
    last = jnp.full((rows, 1), -1, jnp.int32)
    for s, value in enumerate(last_starts(starts_ref, count)):
        last = jnp.where(own == s, value, last)
    fresh = (last < 0).astype(F32)
    masked = jnp.where((other >= last) & (other < own), gram, 0.0)
    base = jnp.sum(keys.astype(F32) * totals_ref[...], axis=-1, keepdims=True)
    scales = jnp.maximum(fresh * base + jnp.sum(masked, axis=-1, keepdims=True), 1.0)
    rates = rates_ref[:, :1]
    current = rates * (values_ref[...] - fresh * probed / scales)
    power = split(masked * (rates / scales))
    current = current - dot3(power, split(current))
    for _ in range(3):
        power = split(dot3(power, power))
        current = current + dot3(power, split(current))
    writes_out[...] = current
    sent_out[...] = current.astype(BF16)


def next_kernel(starts_ref, keys_ref, writes_ref, matrix_ref, totals_ref, matrix_out, totals_out):
    rows = keys_ref.shape[0]
    last = last_starts(starts_ref, rows // MEM)[-1]
    fresh = (last < 0).astype(F32)
    keys = keys_ref[...]
    own = lax.broadcasted_iota(jnp.int32, (rows, 1), 0) // MEM
    writes = jnp.where(own >= last, writes_ref[...], 0.0)
    high, low = split(writes)
    added = dot(high, keys, ((0,), (0,))) + dot(low, keys, ((0,), (0,)))
    matrix_out[...] = (fresh * matrix_ref[...].astype(F32) + added).astype(BF16)
    seen = lax.broadcasted_iota(jnp.int32, (8, rows), 1) // MEM >= last
    sums = dot(seen.astype(F32).astype(BF16), keys)[:1]
    totals_out[...] = fresh * totals_ref[...] + sums


def query_kernel(source_ref, first_ref, second_ref, third_ref, gain_ref, weight_ref, out_ref, rows_ref, normed_ref, arrived):
    @pl.when(pl.program_id(0) == 0)
    def _():
        for number, ref in enumerate((first_ref, second_ref, third_ref)):

            @pl.when(source_ref[0] == number)
            def _(ref=ref):
                copy = pltpu.make_async_copy(ref, rows_ref, arrived)
                copy.start()
                copy.wait()

        normed_ref[...] = normalise(rows_ref[...], gain_ref[...])

    out_ref[...] = phi(dot(normed_ref[...], weight_ref[...])).astype(BF16)


def similarity_kernel(me_ref, starts_ref, queries_ref, keys_ref, totals_ref, high_out, low_out, inverse_out):
    rows = keys_ref.shape[0]
    me = me_ref[0]
    last = jnp.int32(-1)
    for s, value in enumerate(last_starts(starts_ref, rows // MEM)):
        last = jnp.where(me == s, value, last)
    fresh = (last < 0).astype(F32)
    queries = queries_ref[...]
    other = lax.broadcasted_iota(jnp.int32, (1, rows), 1) // MEM
    masked = jnp.where((other >= last) & (other < me), dot(queries, keys_ref[...], ((1,), (1,))), 0.0)
    base = jnp.sum(queries.astype(F32) * totals_ref[...], axis=-1, keepdims=True)
    inverse = 1.0 / jnp.maximum(fresh * base + jnp.sum(masked, axis=-1, keepdims=True), 1.0)
    high_out[...], low_out[...] = split(masked)
    lane = lax.broadcasted_iota(jnp.int32, inverse_out.shape, 1)
    inverse_out[...] = jnp.where(lane < 64, inverse, inverse * fresh)


def read_kernel(place_ref, queries_ref, high_ref, low_ref, inverse_ref, rows_ref, matrix_ref, mine_ref, theirs_ref, *rest):
    out_ref = rest[-1]
    width = mine_ref.shape[2]
    base = dot(queries_ref[...], matrix_ref[...], ((1,), (1,)))
    inverse = inverse_ref[:, :1]
    fresh = inverse_ref[:, 64:65]
    swap = place_ref[1] == 1
    for side in range(2):
        cols = slice(side * width, (side + 1) * width)
        writes = jnp.where(swap == (side == 0), theirs_ref[0], mine_ref[0])
        low = dot(high_ref[...], writes) + dot(low_ref[...], writes)
        out_ref[:, cols] = (rows_ref[:, cols].astype(F32) + (fresh * base[:, cols] + inverse * low)).astype(BF16)


def read_half(half, me, queries, high, low, inverse, entering, matrix, writes, previous=None):
    count, depth = queries.shape
    rows, width = writes[0].shape[1:]
    distance = (jnp.arange(4, dtype=jnp.int32) - me // 4) % 4
    slot_of = jnp.where(distance == 3, 1, jnp.where(distance == 0, 0, distance + 1))
    place = jnp.concatenate([jnp.stack([half, me % 2]), slot_of])
    args = [place, queries, high, low, inverse, entering, matrix, *writes]
    specs = [
        pl.BlockSpec((count, depth), lambda z, p: (0, 0)),
        pl.BlockSpec((count, rows), lambda z, p: (0, 0)),
        pl.BlockSpec((count, rows), lambda z, p: (0, 0)),
        pl.BlockSpec((count, 128), lambda z, p: (0, 0)),
        pl.BlockSpec((count, 2 * width), lambda z, p: (0, 2 * z + p[0])),
        pl.BlockSpec((2 * width, depth), lambda z, p: (z, 0)),
        pl.BlockSpec((1, rows, width), lambda z, p: (p[2 + z], 0, 0)),
        pl.BlockSpec((1, rows, width), lambda z, p: (p[2 + z], 0, 0)),
    ]
    if previous is not None:
        args.append(previous)
        specs.append(pl.BlockSpec(memory_space=pl.ANY))
    return pl.pallas_call(
        read_kernel,
        out_shape=shape(entering.shape, BF16),
        grid_spec=pltpu.PrefetchScalarGridSpec(
            num_scalar_prefetch=1,
            grid=(4,),
            in_specs=specs,
            out_specs=pl.BlockSpec((count, 2 * width), lambda z, p: (0, 2 * z + p[0])),
        ),
        input_output_aliases={} if previous is None else {len(args) - 1: 0},
        interpret=INTERPRET,
    )(*args)


def call(kernel, outs, *args, specs, scratch=()):
    return pl.pallas_call(
        kernel, out_shape=outs, in_specs=list(specs),
        out_specs=jax.tree.map(lambda _: VM, outs), scratch_shapes=scratch, interpret=INTERPRET,
    )(*args)


def shape(dims, kind):
    return jax.ShapeDtypeStruct(dims, kind)


def local(leaving, w_query, w_key, w_value, w_gate, norm_gain, memory_matrix, key_totals, doc_starts):
    me = lax.axis_index("seg").astype(jnp.int32)
    slots = slot_segments(me, offsets())
    pair_slots = slot_segments(me, pair_offsets())
    mine = jnp.full((1,), me)
    leaving, matrix = leaving[0, 0], memory_matrix[0]
    width, features, depth = matrix.shape[0], leaving.shape[1], matrix.shape[1]
    rows = 16 * MEM
    head = shifted(leaving[:MEM])
    across = shifted_across(leaving[:MEM])
    entering = shifted_rows(leaving)
    groups = [[i for i in range(16) if (i // 2) % 2 == y] for y in (0, 1)]
    near = lax.all_gather(matrix, "seg", axis=0, tiled=True, axis_index_groups=groups)
    partner = permute(matrix, "seg", lambda i: i ^ 2)
    away = lax.all_gather(partner, "seg", axis=0, tiled=True, axis_index_groups=groups)

    normed = call(
        norm_kernel, shape((2, MEM, features), BF16), head, across, norm_gain, specs=[VM] * 3
    )
    memory = gather_pairs(normed)
    key_part, values, rates = call(
        kv_kernel,
        (shape((rows, w_key.shape[2]), BF16), shape((rows, width), F32), shape((rows, 128), F32)),
        pair_slots, *memory, w_key[0], w_value[0], w_gate,
        specs=[SM] + [VM] * 11,
    )
    pieces = gather_slots(key_part)
    keys, writes, sent = call(
        solve_kernel,
        (shape((rows, depth), BF16), shape((rows, width), F32), shape((rows, width), BF16)),
        slots, doc_starts, *pieces, values, rates, matrix, key_totals,
        specs=[SM, SM] + [VM] * 8,
    )
    write_slots = gather_slots(sent)
    matrix_next, totals_next = call(
        next_kernel,
        (shape((width, depth), BF16), shape((1, depth), F32)),
        doc_starts, keys, writes, matrix, key_totals,
        specs=[SM] + [VM] * 4,
    )

    count = leaving.shape[0]
    block = depth // 4
    queries, entering = pl.pallas_call(
        query_kernel,
        out_shape=(shape((count, depth), BF16), shape((count, features), BF16)),
        grid=(4,),
        in_specs=[
            SM,
            pl.BlockSpec(memory_space=pl.ANY),
            pl.BlockSpec(memory_space=pl.ANY),
            pl.BlockSpec(memory_space=pl.ANY),
            pl.BlockSpec((1, features), lambda j: (0, 0)),
            pl.BlockSpec((features, block), lambda j: (0, j)),
        ],
        out_specs=(pl.BlockSpec((count, block), lambda j: (0, j)), pl.BlockSpec((count, features), lambda j: (0, 0))),
        scratch_shapes=[pltpu.VMEM((count, features), BF16), pltpu.SemaphoreType.DMA],
        interpret=INTERPRET,
    )(*entering, norm_gain, w_query[0])
    high, low, inverse = call(
        similarity_kernel,
        (shape((count, rows), BF16), shape((count, rows), BF16), shape((count, 128), F32)),
        mine, doc_starts, queries, keys, key_totals,
        specs=[SM, SM] + [VM] * 3,
    )
    half = (me // 2) % 2
    parts = (me, queries, high, low, inverse, entering)
    updated = read_half(half, *parts, near, write_slots[0::2])
    updated = read_half(1 - half, *parts, away, write_slots[1::2], updated)
    return updated[None, None], matrix_next[None], totals_next


def solution(mesh):
    return jax.shard_map(
        local,
        mesh=mesh,
        in_specs=(
            P("seg", "section", None, None),
            P("section", None, None),
            P("section", None, "seg"),
            P("section", None, "seg"),
            P("section", None),
            P("section", None),
            P("section", "seg", None),
            P("section", None),
            P("section", None),
        ),
        out_specs=(P("seg", "section", None, None), P("section", "seg", None), P("section", None)),
        check_vma=False,
    )
```

profile of v0, /device:TPU:1, one launch (start us, length us, event | category | flops | bytes accessed | tf_op | source)
XLA Modules:
  0.0 197.2 jit_solution(9947521662858724317)
XLA Ops:
  8.0 2.2 %collective-permute-start.19 = (bf16[256,2048]{1,0:T(8,128)(2,1)}, bf16[256,2048]{1,0:T(8,128)(2,1)S(1)}, u32[]{:S(2)}, u32[]{:S(2)}) collective-permute-start(bf16[256,2048]{1,0:T(8,128)(2,1)} %bitcast.24), channel_id=1, source_target_pairs={{0,16},{8,24},{16,0},{24,8},{32,48},{40,56},{48,32},{56,40},{64,80... | collective-permute-start | bytes 3145736 | tf_op jit(solution)/shard_map/ppermute | solution.py:22
  10.2 22.8 %collective-permute-done.19 = bf16[256,2048]{1,0:T(8,128)(2,1)S(1)} collective-permute-done((bf16[256,2048]{1,0:T(8,128)(2,1)}, bf16[256,2048]{1,0:T(8,128)(2,1)S(1)}, u32[]{:S(2)}, u32[]{:S(2)}) %collective-permute-start.19) | collective-permute-done | bytes 1048608 | tf_op jit(solution)/shard_map/ppermute | solution.py:22
  33.0 1.1 copy-done.3
  34.1 2.1 %collective-permute-start.2 = (bf16[272,4096]{1,0:T(8,128)(2,1)}, bf16[272,4096]{1,0:T(8,128)(2,1)}, u32[]{:S(2)}, u32[]{:S(2)}) collective-permute-start(bf16[272,4096]{1,0:T(8,128)(2,1)} %bitcast.39), channel_id=1, source_target_pairs={{11,15},{15,11},{19,23},{23,19},{43,47},{47,43},{51,55},{55,51},{7... | collective-permute-start | bytes 6684680 | tf_op jit(solution)/shard_map/ppermute | solution.py:46
  36.2 0.9 slice_bitcast_fusion
  37.1 1.5 collective-permute-start.4
  38.6 2.2 %collective-permute-start.5 = (bf16[16,4096]{1,0:T(8,128)(2,1)S(1)}, bf16[16,4096]{1,0:T(8,128)(2,1)S(1)}, u32[]{:S(2)}, u32[]{:S(2)}) collective-permute-start(bf16[16,4096]{1,0:T(8,128)(2,1)S(1)} %slice_bitcast_fusion), channel_id=1, source_target_pairs={{0,17},{1,18},{2,19},{3,20},{4,21},{5,22},{6,23},{7,16},{8,25},{9,... | collective-permute-start | bytes 393224 | tf_op jit(solution)/shard_map/ppermute | solution.py:36
  40.8 4.0 %collective-permute-done.4.rows_ref = bf16[16,4096]{1,0:T(8,128)(2,1)S(1)} collective-permute-done((bf16[16,4096]{1,0:T(8,128)(2,1)S(1)}, bf16[16,4096]{1,0:T(8,128)(2,1)S(1)}, u32[]{:S(2)}, u32[]{:S(2)}) %collective-permute-start.4) | collective-permute-done | bytes 131104 | tf_op jit(solution)/shard_map/ppermute | solution.py:22
  44.8 3.4 %collective-permute-done.5.across_ref = bf16[16,4096]{1,0:T(8,128)(2,1)S(1)} collective-permute-done((bf16[16,4096]{1,0:T(8,128)(2,1)S(1)}, bf16[16,4096]{1,0:T(8,128)(2,1)S(1)}, u32[]{:S(2)}, u32[]{:S(2)}) %collective-permute-start.5) | collective-permute-done | bytes 131104 | tf_op jit(solution)/shard_map/ppermute | solution.py:36
  48.8 1.8 shard_map.176.refs_0_
  50.7 1.8 collective-permute-start.6
  52.4 2.1 %collective-permute-start.7 = (bf16[2,16,4096]{2,1,0:T(8,128)(2,1)}, bf16[2,16,4096]{2,1,0:T(8,128)(2,1)S(1)}, u32[]{:S(2)}, u32[]{:S(2)}) collective-permute-start(bf16[2,16,4096]{2,1,0:T(8,128)(2,1)} %shard_map.176.refs_0_), channel_id=1, source_target_pairs={{0,96},{8,104},{16,112},{24,120},{32,0},{40,8},{48,16},{56,24},{64... | collective-permute-start | bytes 786440 | tf_op jit(solution)/shard_map/ppermute | solution.py:22
  54.5 1.3 collective-permute-start.8
  55.8 3.1 %collective-permute-start.9 = (bf16[2,16,4096]{2,1,0:T(8,128)(2,1)}, bf16[2,16,4096]{2,1,0:T(8,128)(2,1)S(1)}, u32[]{:S(2)}, u32[]{:S(2)}) collective-permute-start(bf16[2,16,4096]{2,1,0:T(8,128)(2,1)} %shard_map.176.refs_0_), channel_id=1, source_target_pairs={{0,8},{8,0},{16,24},{24,16},{32,40},{40,32},{48,56},{56,48},{64,72... | collective-permute-start | bytes 786440 | tf_op jit(solution)/shard_map/ppermute | solution.py:22
  58.9 7.4 %collective-permute-done.6.refs_1_ = bf16[2,16,4096]{2,1,0:T(8,128)(2,1)S(1)} collective-permute-done((bf16[2,16,4096]{2,1,0:T(8,128)(2,1)}, bf16[2,16,4096]{2,1,0:T(8,128)(2,1)S(1)}, u32[]{:S(2)}, u32[]{:S(2)}) %collective-permute-start.6) | collective-permute-done | bytes 262176 | tf_op jit(solution)/shard_map/ppermute | solution.py:22
  66.3 1.7 collective-permute-start.10
  68.1 3.8 %collective-permute-done.8.refs_3_ = bf16[2,16,4096]{2,1,0:T(8,128)(2,1)S(1)} collective-permute-done((bf16[2,16,4096]{2,1,0:T(8,128)(2,1)}, bf16[2,16,4096]{2,1,0:T(8,128)(2,1)S(1)}, u32[]{:S(2)}, u32[]{:S(2)}) %collective-permute-start.8) | collective-permute-done | bytes 262176 | tf_op jit(solution)/shard_map/ppermute | solution.py:22
  71.9 1.2 collective-permute-start.12
  73.2 3.2 %collective-permute-start = (bf16[272,4096]{1,0:T(8,128)(2,1)}, bf16[272,4096]{1,0:T(8,128)(2,1)S(1)}, u32[]{:S(2)}, u32[]{:S(2)}) collective-permute-start(bf16[272,4096]{1,0:T(8,128)(2,1)} %bitcast.40), channel_id=1, source_target_pairs={{0,1},{1,2},{2,3},{4,5},{5,6},{6,7},{8,9},{9,10},{10,11},{12,13},{... | collective-permute-start | bytes 6684680 | tf_op jit(solution)/shard_map/ppermute | solution.py:46
  76.4 2.1 %collective-permute-start.1 = (bf16[272,4096]{1,0:T(8,128)(2,1)}, bf16[272,4096]{1,0:T(8,128)(2,1)}, u32[]{:S(2)}, u32[]{:S(2)}) collective-permute-start(bf16[272,4096]{1,0:T(8,128)(2,1)} %bitcast.41), channel_id=1, source_target_pairs={{3,4},{7,0},{27,28},{31,24},{35,36},{39,32},{59,60},{63,56},{67,68... | collective-permute-start | bytes 6684680 | tf_op jit(solution)/shard_map/ppermute | solution.py:46
  78.5 1.3 collective-permute-start.3
  79.8 1.2 xor_add_fusion
  81.1 5.1 %shard_map.177 = (bf16[256,128]{1,0:T(8,128)(2,1)}, f32[256,256]{1,0:T(8,128)}, f32[256,128]{1,0:T(8,128)}) custom-call(s32[16]{0:T(128)} %get-tuple-element.31.slots_ref, bf16[2,16,4096]{2,1,0:T(8,128)(2,1)} %shard_map.176.refs_0_, bf16[2,16,4096]{2,1,0:T(8,128)(2,1)} %copy-done.8, bf16[2,16,4096]{2,1,0:T(8,128)(2,1)} %copy-done.9, ...), custom_call_target="tpu_custom_call" | custom-call | tf_op jit(solution)/shard_map/pallas_call | solution.py:279
  86.2 0.9 collective-permute-start.13
  87.1 1.8 collective-permute-start.14
  88.9 4.0 %collective-permute-done.13 = bf16[256,128]{1,0:T(8,128)(2,1)S(1)} collective-permute-done((bf16[256,128]{1,0:T(8,128)(2,1)}, bf16[256,128]{1,0:T(8,128)(2,1)S(1)}, u32[]{:S(2)}, u32[]{:S(2)}) %collective-permute-start.13) | collective-permute-done | bytes 65568 | tf_op jit(solution)/shard_map/ppermute | solution.py:22
  92.8 6.9 %collective-permute-done.15 = bf16[256,128]{1,0:T(8,128)(2,1)S(1)} collective-permute-done((bf16[256,128]{1,0:T(8,128)(2,1)}, bf16[256,128]{1,0:T(8,128)(2,1)S(1)}, u32[]{:S(2)}, u32[]{:S(2)}) %collective-permute-start.15) | collective-permute-done | bytes 65568 | tf_op jit(solution)/shard_map/ppermute | solution.py:22
  99.8 0.9 pad_maximum_fusion.1.a_ref
  100.7 1.1 collective-permute-start.16
  101.8 2.2 %collective-permute-start.17 = (bf16[4,256,128]{2,1,0:T(8,128)(2,1)S(1)}, bf16[4,256,128]{2,1,0:T(8,128)(2,1)S(1)}, u32[]{:S(2)}, u32[]{:S(2)}) collective-permute-start(bf16[4,256,128]{2,1,0:T(8,128)(2,1)S(1)} %pad_maximum_fusion.1.a_ref), channel_id=1, source_target_pairs={{0,8},{8,0},{16,24},{24,16},{32,40},{40,32},{48,56},{56,48},{64,72... | collective-permute-start | bytes 786440 | tf_op jit(solution)/shard_map/ppermute | solution.py:22
  104.0 8.6 %collective-permute-done.16.b_ref = bf16[4,256,128]{2,1,0:T(8,128)(2,1)S(1)} collective-permute-done((bf16[4,256,128]{2,1,0:T(8,128)(2,1)S(1)}, bf16[4,256,128]{2,1,0:T(8,128)(2,1)S(1)}, u32[]{:S(2)}, u32[]{:S(2)}) %collective-permute-start.16) | collective-permute-done | bytes 262176 | tf_op jit(solution)/shard_map/ppermute | solution.py:22
  112.5 2.5 %collective-permute-start.18 = (bf16[4,256,128]{2,1,0:T(8,128)(2,1)S(1)}, bf16[4,256,128]{2,1,0:T(8,128)(2,1)S(1)}, u32[]{:S(2)}, u32[]{:S(2)}) collective-permute-start(bf16[4,256,128]{2,1,0:T(8,128)(2,1)S(1)} %collective-permute-done.16.b_ref), channel_id=1, source_target_pairs={{0,8},{8,0},{16,24},{24,16},{32,40},{40,32},{48,56},{56,48},{64,72... | collective-permute-start | bytes 786440 | tf_op jit(solution)/shard_map/ppermute | solution.py:22
  115.1 1.2 collective-permute-done.18.d_ref
  117.0 5.0 %shard_map.178 = (bf16[256,2048]{1,0:T(8,128)(2,1)}, f32[256,256]{1,0:T(8,128)}, bf16[256,256]{1,0:T(8,128)(2,1)}) custom-call(s32[16]{0:T(128)} %get-tuple-element.32.slots_ref, s32[1,16]{1,0:T(1,128)} %starts_ref.5, bf16[4,256,128]{2,1,0:T(8,128)(2,1)} %copy-done.2, bf16[4,256,128]{2,1,0:T(8,128)(2,1)} %copy-done.5, bf16[4,256,128]{2,1,0:T(8,128)(2,1)} %copy-done.6, ...), custom_call_target="tpu_custom_call" | custom-call | tf_op jit(solution)/shard_map/pallas_call | solution.py:279
  122.1 2.6 %collective-permute-start.21 = (bf16[256,256]{1,0:T(8,128)(2,1)}, bf16[256,256]{1,0:T(8,128)(2,1)S(1)}, u32[]{:S(2)}, u32[]{:S(2)}) collective-permute-start(bf16[256,256]{1,0:T(8,128)(2,1)} %get-tuple-element.25), channel_id=1, source_target_pairs={{0,96},{8,104},{16,112},{24,120},{32,0},{40,8},{48,16},{56,24},{64... | collective-permute-start | bytes 393224 | tf_op jit(solution)/shard_map/ppermute | solution.py:22
  124.7 3.6 %collective-permute-done.20 = bf16[256,256]{1,0:T(8,128)(2,1)S(1)} collective-permute-done((bf16[256,256]{1,0:T(8,128)(2,1)}, bf16[256,256]{1,0:T(8,128)(2,1)S(1)}, u32[]{:S(2)}, u32[]{:S(2)}) %collective-permute-start.20) | collective-permute-done | bytes 131104 | tf_op jit(solution)/shard_map/ppermute | solution.py:22
  128.9 4.9 %collective-permute-done.22 = bf16[256,256]{1,0:T(8,128)(2,1)S(1)} collective-permute-done((bf16[256,256]{1,0:T(8,128)(2,1)}, bf16[256,256]{1,0:T(8,128)(2,1)S(1)}, u32[]{:S(2)}, u32[]{:S(2)}) %collective-permute-start.22) | collective-permute-done | bytes 131104 | tf_op jit(solution)/shard_map/ppermute | solution.py:22
  133.9 1.0 pad_maximum_fusion.mine_ref
  134.8 1.1 collective-permute-start.23
  135.9 2.5 %collective-permute-start.25 = (bf16[4,256,256]{2,1,0:T(8,128)(2,1)S(1)}, bf16[4,256,256]{2,1,0:T(8,128)(2,1)}, u32[]{:S(2)}, u32[]{:S(2)}) collective-permute-start(bf16[4,256,256]{2,1,0:T(8,128)(2,1)S(1)} %pad_maximum_fusion.mine_ref), channel_id=1, source_target_pairs={{0,8},{8,0},{16,24},{24,16},{32,40},{40,32},{48,56},{56,48},{64,72... | collective-permute-start | bytes 1572872 | tf_op jit(solution)/shard_map/ppermute | solution.py:22
  138.4 7.8 %collective-permute-done.23.mine_ref = bf16[4,256,256]{2,1,0:T(8,128)(2,1)S(1)} collective-permute-done((bf16[4,256,256]{2,1,0:T(8,128)(2,1)S(1)}, bf16[4,256,256]{2,1,0:T(8,128)(2,1)S(1)}, u32[]{:S(2)}, u32[]{:S(2)}) %collective-permute-start.23) | collective-permute-done | bytes 524320 | tf_op jit(solution)/shard_map/ppermute | solution.py:22
  146.2 3.0 %collective-permute-start.24 = (bf16[4,256,256]{2,1,0:T(8,128)(2,1)S(1)}, bf16[4,256,256]{2,1,0:T(8,128)(2,1)}, u32[]{:S(2)}, u32[]{:S(2)}) collective-permute-start(bf16[4,256,256]{2,1,0:T(8,128)(2,1)S(1)} %collective-permute-done.23.mine_ref), channel_id=1, source_target_pairs={{0,8},{8,0},{16,24},{24,16},{32,40},{40,32},{48,56},{56,48},{64,72... | collective-permute-start | bytes 1572872 | tf_op jit(solution)/shard_map/ppermute | solution.py:22
  151.2 3.4 %shard_map.182 = (bf16[256,2048]{1,0:T(8,128)(2,1)}, f32[1,2048]{1,0:T(1,128)}) custom-call(s32[1,16]{1,0:T(1,128)} %starts_ref.5, bf16[256,2048]{1,0:T(8,128)(2,1)} %get-tuple-element.20.keys_ref, f32[256,256]{1,0:T(8,128)} %get-tuple-element.26.writes_ref, bf16[256,2048]{1,0:T(8,128)(2,1)} %bitcast.26, f32[1,2048]{1,0:T(1,128)} %totals_ref.5), custom_call_target="tpu_custom_call" | custom-call | tf_op jit(solution)/shard_map/pallas_call | solution.py:279
  154.6 1.3 copy-done
  155.9 13.5 %shard_map.175 = (bf16[272,2048]{1,0:T(8,128)(2,1)}, bf16[272,4096]{1,0:T(8,128)(2,1)}) custom-call(s32[1]{0:T(128)} %bitcast.2.source_ref, bf16[272,4096]{1,0:T(8,128)(2,1)} %copy-done, bf16[272,4096]{1,0:T(8,128)(2,1)} %collective-permute-done.1.second_ref, bf16[272,4096]{1,0:T(8,128)(2,1)} %collective-permute-done.3.third_ref, bf16[1,4096]{1,0:T(2,128)(2,1)} %gain_ref.3, ...), custom_call_target="tpu_custom_call" | custom-call | tf_op jit(solution)/shard_map/pallas_call | solution.py:332
  169.4 2.9 %shard_map.179 = (bf16[272,256]{1,0:T(8,128)(2,1)}, bf16[272,256]{1,0:T(8,128)(2,1)}, f32[272,128]{1,0:T(8,128)}) custom-call(s32[1]{0:T(128)} %bitcast.5.me_ref, s32[1,16]{1,0:T(1,128)} %starts_ref.5, bf16[272,2048]{1,0:T(8,128)(2,1)} %get-tuple-element.16.queries_ref, bf16[256,2048]{1,0:T(8,128)(2,1)} %get-tuple-element.20.keys_ref, f32[1,2048]{1,0:T(1,128)} %totals_ref.5), custom_call_target="tpu_custom_call" | custom-call | tf_op jit(solution)/shard_map/pallas_call | solution.py:279
  172.3 9.0 %shard_map.180.rest_0_ = bf16[272,4096]{1,0:T(8,128)(2,1)} custom-call(s32[6]{0:T(128)} %get-tuple-element.29.place_ref, bf16[272,2048]{1,0:T(8,128)(2,1)} %get-tuple-element.16.queries_ref, bf16[272,256]{1,0:T(8,128)(2,1)} %get-tuple-element.21.high_ref, bf16[272,256]{1,0:T(8,128)(2,1)} %get-tuple-element.22.low_ref, ...), custom_call_target="tpu_custom_call" | custom-call | tf_op jit(solution)/shard_map/pallas_call | solution.py:264
  181.3 9.0 %shard_map.181 = bf16[272,4096]{1,0:T(8,128)(2,1)} custom-call(s32[6]{0:T(128)} %get-tuple-element.30.place_ref, bf16[272,2048]{1,0:T(8,128)(2,1)} %get-tuple-element.16.queries_ref, bf16[272,256]{1,0:T(8,128)(2,1)} %get-tuple-element.21.high_ref, bf16[272,256]{1,0:T(8,128)(2,1)} %get-tuple-element.22.low_ref, ...), custom_call_target="tpu_custom_call", output_to_operand_aliasing={{}: (9, {})} | custom-call | tf_op jit(solution)/shard_map/pallas_call | solution.py:264
  (65 shorter events, 4.4 us)
Async XLA Ops:
  7.2 72.6 %copy-start.15 = (s32[16]{0:T(128)S(1)}, s32[16]{0:T(128)}, u32[]{:S(2)}) copy-start(s32[16]{0:T(128)} %constant.121.clone) | copy-start | bytes 196
  7.2 72.6 %copy-start.16 = (s32[16]{0:T(128)S(1)}, s32[16]{0:T(128)}, u32[]{:S(2)}) copy-start(s32[16]{0:T(128)} %constant.122.clone) | copy-start | bytes 196
  7.2 72.6 %copy-start.17 = (s32[16]{0:T(128)S(1)}, s32[16]{0:T(128)}, u32[]{:S(2)}) copy-start(s32[16]{0:T(128)} %constant.123.clone) | copy-start | bytes 196
  7.2 72.6 %copy-start.18 = (s32[16]{0:T(128)S(1)}, s32[16]{0:T(128)}, u32[]{:S(2)}) copy-start(s32[16]{0:T(128)} %constant.124.clone) | copy-start | bytes 196
  7.2 165.1 %all-gather.6.cloned.1.call-start = ((), (), s32[]{:S(2)}) async-start(), calls=%async_computation.1 | async-start | bytes 9437184 | tf_op jit(solution)/shard_map/all_gather | solution.py:301
  7.9 173.4 %all-gather.4.cloned.1.call-start = ((), (), s32[]{:S(2)}) async-start(), calls=%async_computation | async-start | bytes 9437184 | tf_op jit(solution)/shard_map/all_gather | solution.py:303
  8.0 25.0 %collective-permute-start.19 = (bf16[256,2048]{1,0:T(8,128)(2,1)}, bf16[256,2048]{1,0:T(8,128)(2,1)S(1)}, u32[]{:S(2)}, u32[]{:S(2)}) collective-permute-start(bf16[256,2048]{1,0:T(8,128)(2,1)} %bitcast.24), channel_id=1, source_target_pairs={{0,16},{8,24},{16,0},{24,8},{32,48},{40,56},{48,32},{56,40},{64,80... | collective-permute-start | bytes 3145736 | tf_op jit(solution)/shard_map/ppermute | solution.py:22
  33.0 1.1 copy-start.3
  34.1 44.3 %collective-permute-start.2 = (bf16[272,4096]{1,0:T(8,128)(2,1)}, bf16[272,4096]{1,0:T(8,128)(2,1)}, u32[]{:S(2)}, u32[]{:S(2)}) collective-permute-start(bf16[272,4096]{1,0:T(8,128)(2,1)} %bitcast.39), channel_id=1, source_target_pairs={{11,15},{15,11},{19,23},{23,19},{43,47},{47,43},{51,55},{55,51},{7... | collective-permute-start | bytes 6684680 | tf_op jit(solution)/shard_map/ppermute | solution.py:46
  37.1 7.7 %collective-permute-start.4 = (bf16[16,4096]{1,0:T(8,128)(2,1)S(1)}, bf16[16,4096]{1,0:T(8,128)(2,1)S(1)}, u32[]{:S(2)}, u32[]{:S(2)}) collective-permute-start(bf16[16,4096]{1,0:T(8,128)(2,1)S(1)} %slice_bitcast_fusion), channel_id=1, source_target_pairs={{0,1},{1,2},{2,3},{3,4},{4,5},{5,6},{6,7},{7,0},{8,9},{9,10},{10,1... | collective-permute-start | bytes 393224 | tf_op jit(solution)/shard_map/ppermute | solution.py:22
  38.6 9.5 %collective-permute-start.5 = (bf16[16,4096]{1,0:T(8,128)(2,1)S(1)}, bf16[16,4096]{1,0:T(8,128)(2,1)S(1)}, u32[]{:S(2)}, u32[]{:S(2)}) collective-permute-start(bf16[16,4096]{1,0:T(8,128)(2,1)S(1)} %slice_bitcast_fusion), channel_id=1, source_target_pairs={{0,17},{1,18},{2,19},{3,20},{4,21},{5,22},{6,23},{7,16},{8,25},{9,... | collective-permute-start | bytes 393224 | tf_op jit(solution)/shard_map/ppermute | solution.py:36
  44.8 3.4 %copy-start.13 = (bf16[16,4096]{1,0:T(8,128)(2,1)}, bf16[16,4096]{1,0:T(8,128)(2,1)S(1)}, u32[]{:S(2)}) copy-start(bf16[16,4096]{1,0:T(8,128)(2,1)S(1)} %collective-permute-done.4.rows_ref) | copy-start | bytes 393220
  48.2 0.6 copy-start.14
  50.7 15.6 %collective-permute-start.6 = (bf16[2,16,4096]{2,1,0:T(8,128)(2,1)}, bf16[2,16,4096]{2,1,0:T(8,128)(2,1)S(1)}, u32[]{:S(2)}, u32[]{:S(2)}) collective-permute-start(bf16[2,16,4096]{2,1,0:T(8,128)(2,1)} %shard_map.176.refs_0_), channel_id=1, source_target_pairs={{0,32},{8,40},{16,48},{24,56},{32,64},{40,72},{48,80},{56,88},{64,... | collective-permute-start | bytes 786440 | tf_op jit(solution)/shard_map/ppermute | solution.py:22
  52.4 15.6 %collective-permute-start.7 = (bf16[2,16,4096]{2,1,0:T(8,128)(2,1)}, bf16[2,16,4096]{2,1,0:T(8,128)(2,1)S(1)}, u32[]{:S(2)}, u32[]{:S(2)}) collective-permute-start(bf16[2,16,4096]{2,1,0:T(8,128)(2,1)} %shard_map.176.refs_0_), channel_id=1, source_target_pairs={{0,96},{8,104},{16,112},{24,120},{32,0},{40,8},{48,16},{56,24},{64... | collective-permute-start | bytes 786440 | tf_op jit(solution)/shard_map/ppermute | solution.py:22
  54.5 17.4 %collective-permute-start.8 = (bf16[2,16,4096]{2,1,0:T(8,128)(2,1)}, bf16[2,16,4096]{2,1,0:T(8,128)(2,1)S(1)}, u32[]{:S(2)}, u32[]{:S(2)}) collective-permute-start(bf16[2,16,4096]{2,1,0:T(8,128)(2,1)} %shard_map.176.refs_0_), channel_id=1, source_target_pairs={{0,64},{8,72},{16,80},{24,88},{32,96},{40,104},{48,112},{56,120},{... | collective-permute-start | bytes 786440 | tf_op jit(solution)/shard_map/ppermute | solution.py:22
  55.8 17.4 %collective-permute-start.9 = (bf16[2,16,4096]{2,1,0:T(8,128)(2,1)}, bf16[2,16,4096]{2,1,0:T(8,128)(2,1)S(1)}, u32[]{:S(2)}, u32[]{:S(2)}) collective-permute-start(bf16[2,16,4096]{2,1,0:T(8,128)(2,1)} %shard_map.176.refs_0_), channel_id=1, source_target_pairs={{0,8},{8,0},{16,24},{24,16},{32,40},{40,32},{48,56},{56,48},{64,72... | collective-permute-start | bytes 786440 | tf_op jit(solution)/shard_map/ppermute | solution.py:22
  66.3 14.7 %copy-start.8 = (bf16[2,16,4096]{2,1,0:T(8,128)(2,1)}, bf16[2,16,4096]{2,1,0:T(8,128)(2,1)S(1)}, u32[]{:S(2)}) copy-start(bf16[2,16,4096]{2,1,0:T(8,128)(2,1)S(1)} %collective-permute-done.6.refs_1_) | copy-start | bytes 786436
  66.3 10.1 %collective-permute-start.10 = (bf16[2,16,4096]{2,1,0:T(8,128)(2,1)S(1)}, bf16[2,16,4096]{2,1,0:T(8,128)(2,1)S(1)}, u32[]{:S(2)}, u32[]{:S(2)}) collective-permute-start(bf16[2,16,4096]{2,1,0:T(8,128)(2,1)S(1)} %collective-permute-done.6.refs_1_), channel_id=1, source_target_pairs={{0,8},{8,0},{16,24},{24,16},{32,40},{40,32},{48,56},{56,48},{64,72... | collective-permute-start | bytes 786440 | tf_op jit(solution)/shard_map/ppermute | solution.py:22
  68.0 13.0 %copy-start.9 = (bf16[2,16,4096]{2,1,0:T(8,128)(2,1)}, bf16[2,16,4096]{2,1,0:T(8,128)(2,1)S(1)}, u32[]{:S(2)}) copy-start(bf16[2,16,4096]{2,1,0:T(8,128)(2,1)S(1)} %collective-permute-done.7.refs_2_) | copy-start | bytes 786436
  68.0 13.0 %collective-permute-start.11 = (bf16[2,16,4096]{2,1,0:T(8,128)(2,1)S(1)}, bf16[2,16,4096]{2,1,0:T(8,128)(2,1)}, u32[]{:S(2)}, u32[]{:S(2)}) collective-permute-start(bf16[2,16,4096]{2,1,0:T(8,128)(2,1)S(1)} %collective-permute-done.7.refs_2_), channel_id=1, source_target_pairs={{0,8},{8,0},{16,24},{24,16},{32,40},{40,32},{48,56},{56,48},{64,72... | collective-permute-start | bytes 786440 | tf_op jit(solution)/shard_map/ppermute | solution.py:22
  71.9 9.1 %copy-start.10 = (bf16[2,16,4096]{2,1,0:T(8,128)(2,1)}, bf16[2,16,4096]{2,1,0:T(8,128)(2,1)S(1)}, u32[]{:S(2)}) copy-start(bf16[2,16,4096]{2,1,0:T(8,128)(2,1)S(1)} %collective-permute-done.8.refs_3_) | copy-start | bytes 786436
  71.9 9.1 %collective-permute-start.12 = (bf16[2,16,4096]{2,1,0:T(8,128)(2,1)S(1)}, bf16[2,16,4096]{2,1,0:T(8,128)(2,1)}, u32[]{:S(2)}, u32[]{:S(2)}) collective-permute-start(bf16[2,16,4096]{2,1,0:T(8,128)(2,1)S(1)} %collective-permute-done.8.refs_3_), channel_id=1, source_target_pairs={{0,8},{8,0},{16,24},{24,16},{32,40},{40,32},{48,56},{56,48},{64,72... | collective-permute-start | bytes 786440 | tf_op jit(solution)/shard_map/ppermute | solution.py:22
  73.2 7.9 %copy-start.11 = (bf16[2,16,4096]{2,1,0:T(8,128)(2,1)}, bf16[2,16,4096]{2,1,0:T(8,128)(2,1)S(1)}, u32[]{:S(2)}) copy-start(bf16[2,16,4096]{2,1,0:T(8,128)(2,1)S(1)} %collective-permute-done.9.refs_4_) | copy-start | bytes 786436
  73.2 81.4 %collective-permute-start = (bf16[272,4096]{1,0:T(8,128)(2,1)}, bf16[272,4096]{1,0:T(8,128)(2,1)S(1)}, u32[]{:S(2)}, u32[]{:S(2)}) collective-permute-start(bf16[272,4096]{1,0:T(8,128)(2,1)} %bitcast.40), channel_id=1, source_target_pairs={{0,1},{1,2},{2,3},{4,5},{5,6},{6,7},{8,9},{9,10},{10,11},{12,13},{... | collective-permute-start | bytes 6684680 | tf_op jit(solution)/shard_map/ppermute | solution.py:46
  76.4 4.7 %copy-start.12 = (bf16[2,16,4096]{2,1,0:T(8,128)(2,1)}, bf16[2,16,4096]{2,1,0:T(8,128)(2,1)S(1)}, u32[]{:S(2)}) copy-start(bf16[2,16,4096]{2,1,0:T(8,128)(2,1)S(1)} %collective-permute-done.10.refs_5_) | copy-start | bytes 786436
  76.4 78.2 %collective-permute-start.1 = (bf16[272,4096]{1,0:T(8,128)(2,1)}, bf16[272,4096]{1,0:T(8,128)(2,1)}, u32[]{:S(2)}, u32[]{:S(2)}) collective-permute-start(bf16[272,4096]{1,0:T(8,128)(2,1)} %bitcast.41), channel_id=1, source_target_pairs={{3,4},{7,0},{27,28},{31,24},{35,36},{39,32},{59,60},{63,56},{67,68... | collective-permute-start | bytes 6684680 | tf_op jit(solution)/shard_map/ppermute | solution.py:46
  78.5 76.1 %collective-permute-start.3 = (bf16[272,4096]{1,0:T(8,128)(2,1)}, bf16[272,4096]{1,0:T(8,128)(2,1)}, u32[]{:S(2)}, u32[]{:S(2)}) collective-permute-start(bf16[272,4096]{1,0:T(8,128)(2,1)} %collective-permute-done.2), channel_id=1, source_target_pairs={{11,8},{15,12},{19,16},{23,20},{43,40},{47,44},{51,48},{55,52},{75... | collective-permute-start | bytes 6684680 | tf_op jit(solution)/shard_map/ppermute | solution.py:46
  86.2 63.1 %copy-start.19 = (s32[8]{0:T(128)S(1)}, s32[8]{0:T(128)}, u32[]{:S(2)}) copy-start(s32[8]{0:T(128)} %constant.126.clone) | copy-start | bytes 100
  86.2 6.6 %collective-permute-start.13 = (bf16[256,128]{1,0:T(8,128)(2,1)}, bf16[256,128]{1,0:T(8,128)(2,1)S(1)}, u32[]{:S(2)}, u32[]{:S(2)}) collective-permute-start(bf16[256,128]{1,0:T(8,128)(2,1)} %get-tuple-element.17), channel_id=1, source_target_pairs={{0,32},{8,40},{16,48},{24,56},{32,64},{40,72},{48,80},{56,88},{64,... | collective-permute-start | bytes 196616 | tf_op jit(solution)/shard_map/ppermute | solution.py:22
  87.1 5.7 %collective-permute-start.14 = (bf16[256,128]{1,0:T(8,128)(2,1)}, bf16[256,128]{1,0:T(8,128)(2,1)S(1)}, u32[]{:S(2)}, u32[]{:S(2)}) collective-permute-start(bf16[256,128]{1,0:T(8,128)(2,1)} %get-tuple-element.17), channel_id=1, source_target_pairs={{0,96},{8,104},{16,112},{24,120},{32,0},{40,8},{48,16},{56,24},{64... | collective-permute-start | bytes 196616 | tf_op jit(solution)/shard_map/ppermute | solution.py:22
  92.8 7.0 %collective-permute-start.15 = (bf16[256,128]{1,0:T(8,128)(2,1)}, bf16[256,128]{1,0:T(8,128)(2,1)S(1)}, u32[]{:S(2)}, u32[]{:S(2)}) collective-permute-start(bf16[256,128]{1,0:T(8,128)(2,1)} %get-tuple-element.17), channel_id=1, source_target_pairs={{0,64},{8,72},{16,80},{24,88},{32,96},{40,104},{48,112},{56,120},{... | collective-permute-start | bytes 196616 | tf_op jit(solution)/shard_map/ppermute | solution.py:22
  100.7 15.6 %copy-start.2 = (bf16[4,256,128]{2,1,0:T(8,128)(2,1)}, bf16[4,256,128]{2,1,0:T(8,128)(2,1)S(1)}, u32[]{:S(2)}) copy-start(bf16[4,256,128]{2,1,0:T(8,128)(2,1)S(1)} %pad_maximum_fusion.1.a_ref) | copy-start | bytes 786436
  100.7 11.9 %collective-permute-start.16 = (bf16[4,256,128]{2,1,0:T(8,128)(2,1)S(1)}, bf16[4,256,128]{2,1,0:T(8,128)(2,1)S(1)}, u32[]{:S(2)}, u32[]{:S(2)}) collective-permute-start(bf16[4,256,128]{2,1,0:T(8,128)(2,1)S(1)} %pad_maximum_fusion.1.a_ref), channel_id=1, source_target_pairs={{0,16},{8,24},{16,0},{24,8},{32,48},{40,56},{48,32},{56,40},{64,80... | collective-permute-start | bytes 786440 | tf_op jit(solution)/shard_map/ppermute | solution.py:22
  101.8 13.3 %collective-permute-start.17 = (bf16[4,256,128]{2,1,0:T(8,128)(2,1)S(1)}, bf16[4,256,128]{2,1,0:T(8,128)(2,1)S(1)}, u32[]{:S(2)}, u32[]{:S(2)}) collective-permute-start(bf16[4,256,128]{2,1,0:T(8,128)(2,1)S(1)} %pad_maximum_fusion.1.a_ref), channel_id=1, source_target_pairs={{0,8},{8,0},{16,24},{24,16},{32,40},{40,32},{48,56},{56,48},{64,72... | collective-permute-start | bytes 786440 | tf_op jit(solution)/shard_map/ppermute | solution.py:22
  112.5 3.7 %copy-start.5 = (bf16[4,256,128]{2,1,0:T(8,128)(2,1)}, bf16[4,256,128]{2,1,0:T(8,128)(2,1)S(1)}, u32[]{:S(2)}) copy-start(bf16[4,256,128]{2,1,0:T(8,128)(2,1)S(1)} %collective-permute-done.16.b_ref) | copy-start | bytes 786436
  112.5 3.7 %collective-permute-start.18 = (bf16[4,256,128]{2,1,0:T(8,128)(2,1)S(1)}, bf16[4,256,128]{2,1,0:T(8,128)(2,1)S(1)}, u32[]{:S(2)}, u32[]{:S(2)}) collective-permute-start(bf16[4,256,128]{2,1,0:T(8,128)(2,1)S(1)} %collective-permute-done.16.b_ref), channel_id=1, source_target_pairs={{0,8},{8,0},{16,24},{24,16},{32,40},{40,32},{48,56},{56,48},{64,72... | collective-permute-start | bytes 786440 | tf_op jit(solution)/shard_map/ppermute | solution.py:22
  115.1 1.2 copy-start.6
  116.3 0.7 copy-start.7
  122.0 6.3 %collective-permute-start.20 = (bf16[256,256]{1,0:T(8,128)(2,1)}, bf16[256,256]{1,0:T(8,128)(2,1)S(1)}, u32[]{:S(2)}, u32[]{:S(2)}) collective-permute-start(bf16[256,256]{1,0:T(8,128)(2,1)} %get-tuple-element.25), channel_id=1, source_target_pairs={{0,32},{8,40},{16,48},{24,56},{32,64},{40,72},{48,80},{56,88},{64,... | collective-permute-start | bytes 393224 | tf_op jit(solution)/shard_map/ppermute | solution.py:22
  122.1 6.8 %collective-permute-start.21 = (bf16[256,256]{1,0:T(8,128)(2,1)}, bf16[256,256]{1,0:T(8,128)(2,1)S(1)}, u32[]{:S(2)}, u32[]{:S(2)}) collective-permute-start(bf16[256,256]{1,0:T(8,128)(2,1)} %get-tuple-element.25), channel_id=1, source_target_pairs={{0,96},{8,104},{16,112},{24,120},{32,0},{40,8},{48,16},{56,24},{64... | collective-permute-start | bytes 393224 | tf_op jit(solution)/shard_map/ppermute | solution.py:22
  128.3 5.5 %collective-permute-start.22 = (bf16[256,256]{1,0:T(8,128)(2,1)}, bf16[256,256]{1,0:T(8,128)(2,1)S(1)}, u32[]{:S(2)}, u32[]{:S(2)}) collective-permute-start(bf16[256,256]{1,0:T(8,128)(2,1)} %get-tuple-element.25), channel_id=1, source_target_pairs={{0,64},{8,72},{16,80},{24,88},{32,96},{40,104},{48,112},{56,120},{... | collective-permute-start | bytes 393224 | tf_op jit(solution)/shard_map/ppermute | solution.py:22
  134.8 34.6 %copy-start.1 = (bf16[4,256,256]{2,1,0:T(8,128)(2,1)}, bf16[4,256,256]{2,1,0:T(8,128)(2,1)S(1)}, u32[]{:S(2)}) copy-start(bf16[4,256,256]{2,1,0:T(8,128)(2,1)S(1)} %pad_maximum_fusion.mine_ref) | copy-start | bytes 1572868
  134.8 11.4 %collective-permute-start.23 = (bf16[4,256,256]{2,1,0:T(8,128)(2,1)S(1)}, bf16[4,256,256]{2,1,0:T(8,128)(2,1)S(1)}, u32[]{:S(2)}, u32[]{:S(2)}) collective-permute-start(bf16[4,256,256]{2,1,0:T(8,128)(2,1)S(1)} %pad_maximum_fusion.mine_ref), channel_id=1, source_target_pairs={{0,16},{8,24},{16,0},{24,8},{32,48},{40,56},{48,32},{56,40},{64,80... | collective-permute-start | bytes 1572872 | tf_op jit(solution)/shard_map/ppermute | solution.py:22
  135.9 36.4 %collective-permute-start.25 = (bf16[4,256,256]{2,1,0:T(8,128)(2,1)S(1)}, bf16[4,256,256]{2,1,0:T(8,128)(2,1)}, u32[]{:S(2)}, u32[]{:S(2)}) collective-permute-start(bf16[4,256,256]{2,1,0:T(8,128)(2,1)S(1)} %pad_maximum_fusion.mine_ref), channel_id=1, source_target_pairs={{0,8},{8,0},{16,24},{24,16},{32,40},{40,32},{48,56},{56,48},{64,72... | collective-permute-start | bytes 1572872 | tf_op jit(solution)/shard_map/ppermute | solution.py:22
  146.2 23.2 %copy-start.4 = (bf16[4,256,256]{2,1,0:T(8,128)(2,1)}, bf16[4,256,256]{2,1,0:T(8,128)(2,1)S(1)}, u32[]{:S(2)}) copy-start(bf16[4,256,256]{2,1,0:T(8,128)(2,1)S(1)} %collective-permute-done.23.mine_ref) | copy-start | bytes 1572868
  146.2 35.1 %collective-permute-start.24 = (bf16[4,256,256]{2,1,0:T(8,128)(2,1)S(1)}, bf16[4,256,256]{2,1,0:T(8,128)(2,1)}, u32[]{:S(2)}, u32[]{:S(2)}) collective-permute-start(bf16[4,256,256]{2,1,0:T(8,128)(2,1)S(1)} %collective-permute-done.23.mine_ref), channel_id=1, source_target_pairs={{0,8},{8,0},{16,24},{24,16},{32,40},{40,32},{48,56},{56,48},{64,72... | collective-permute-start | bytes 1572872 | tf_op jit(solution)/shard_map/ppermute | solution.py:22
  154.6 1.4 copy-start
Sparse Core Ops, SparseCore 0:
  9.7 58.2 all-gather.5
  69.8 57.8 all-gather.3
where the time goes:
time: 198 us; the launch traced here: 197 us
  waiting for transfers between devices  79.1 us (40%)
  Pallas kernels  49.7 us (25%)
  starting transfers between devices  44.3 us (22%)
  between operations  14.9 us (8%)
  local copies, waits for them, and re-layouts  4.78 us (2%)
  other arithmetic  4.33 us (2%)
    ppermute x21, waiting for transfers between devices, permute(): return lax.ppermute(block, axis, [(i, target(i)) for i in range(size)])  75.1 us
    ppermute x21, starting transfers between devices, permute(): return lax.ppermute(block, axis, [(i, target(i)) for i in range(size)])  33.4 us
    pallas_call x5, Pallas kernels, call(): pl.pallas_call(kernel, out_shape=outs, in_specs=list(specs), out_specs=ja...  18.2 us
    pallas_call x2, Pallas kernels, read_half(): pl.pallas_call(read_kernel, out_shape=shape(entering.shape, BF16), grid_s...  18 us
    pallas_call x1, Pallas kernels, local(): pl.pallas_call(query_kernel, out_shape=(shape((count, depth), BF16), shap...  13.5 us
    ppermute x4, starting transfers between devices, send(): lax.ppermute(part, ('seg', 'section'), [(s * wide + p, s * wide + q) for...  8.62 us
  transfers between devices with their start and end apart: 28, of which 12 were waited for; matrix products, arithmetic and copies ran while one was open for 3% of the time, Pallas kernels for 21%

commit v1 on v0

--- a/solution.py
+++ b/solution.py
@@ -1,3 +1,5 @@
+import functools
+
 import jax
 import jax.numpy as jnp
 from jax import lax
@@ -132,7 +134,7 @@
 
 
 def kv_kernel(slots_ref, *refs):
-    pairs, (key_ref, value_ref, gate_ref, key_out, value_out, gate_out) = refs[:8], refs[8:]
+    pairs, (key_ref, value_ref, gate_ref, key_out, value_out, sent_out, gate_out) = refs[:8], refs[8:]
     count = 16
     memory = jnp.concatenate([ref[...] for ref in pairs], axis=0)
     memory = memory.reshape(count * MEM, memory.shape[2])
@@ -140,16 +142,18 @@
     values = dot(memory, value_ref[...])
     gate = jnp.broadcast_to(gate_ref[...], (8, gate_ref.shape[1]))
     rates = jax.nn.sigmoid(dot(memory, gate, ((1,), (1,))))[:, :1]
+    values = rates * values
     rates = jnp.broadcast_to(rates, (count * MEM, 128))
     for slot in range(count):
         rows = pl.ds(pl.multiple_of(slots_ref[slot] * MEM, MEM), MEM)
         part = slice(slot * MEM, (slot + 1) * MEM)
         key_out[rows, :] = keys[part]
         value_out[rows, :] = values[part]
+        sent_out[rows, :] = values[part].astype(BF16)
         gate_out[rows, :] = rates[part]
 
 
-def solve_kernel(slots_ref, starts_ref, a_ref, b_ref, c_ref, d_ref, values_ref, rates_ref, matrix_ref, totals_ref, keys_out, writes_out, sent_out):
+def solve_kernel(slots_ref, starts_ref, a_ref, b_ref, c_ref, d_ref, values_ref, rates_ref, matrix_ref, totals_ref, keys_out, writes_out, inverse_out, scaled_out):
     pieces = (a_ref, b_ref, c_ref, d_ref)
     each, rows, width = a_ref.shape
     count = 4 * each
@@ -169,14 +173,20 @@
     base = jnp.sum(keys.astype(F32) * totals_ref[...], axis=-1, keepdims=True)
     scales = jnp.maximum(fresh * base + jnp.sum(masked, axis=-1, keepdims=True), 1.0)
     rates = rates_ref[:, :1]
-    current = rates * (values_ref[...] - fresh * probed / scales)
+    weights = fresh * rates / scales
+    same = lax.broadcasted_iota(jnp.int32, (rows, rows), 0) == lax.broadcasted_iota(jnp.int32, (rows, rows), 1)
+    current = jnp.concatenate(
+        [values_ref[...] - weights * probed, same.astype(F32), jnp.where(same, weights, 0.0)], axis=1
+    )
     power = split(masked * (rates / scales))
     current = current - dot3(power, split(current))
     for _ in range(3):
         power = split(dot3(power, power))
         current = current + dot3(power, split(current))
-    writes_out[...] = current
-    sent_out[...] = current.astype(BF16)
+    wide = current.shape[1] - 2 * rows
+    writes_out[...] = current[:, :wide]
+    for out, part in ((inverse_out, current[:, wide : wide + rows]), (scaled_out, current[:, wide + rows :])):
+        out[...] = part.astype(BF16)
 
 
 def next_kernel(starts_ref, keys_ref, writes_ref, matrix_ref, totals_ref, matrix_out, totals_out):
@@ -186,22 +196,21 @@
     keys = keys_ref[...]
     own = lax.broadcasted_iota(jnp.int32, (rows, 1), 0) // MEM
     writes = jnp.where(own >= last, writes_ref[...], 0.0)
-    high, low = split(writes)
-    added = dot(high, keys, ((0,), (0,))) + dot(low, keys, ((0,), (0,)))
+    added = dot(writes.astype(BF16), keys, ((0,), (0,)))
     matrix_out[...] = (fresh * matrix_ref[...].astype(F32) + added).astype(BF16)
     seen = lax.broadcasted_iota(jnp.int32, (8, rows), 1) // MEM >= last
     sums = dot(seen.astype(F32).astype(BF16), keys)[:1]
     totals_out[...] = fresh * totals_ref[...] + sums
 
 
-def query_kernel(source_ref, first_ref, second_ref, third_ref, gain_ref, weight_ref, out_ref, rows_ref, normed_ref, arrived):
+def query_kernel(source_ref, first_ref, second_ref, third_ref, gain_ref, weight_ref, out_ref, rows_ref, normed_ref, landed):
     @pl.when(pl.program_id(0) == 0)
     def _():
         for number, ref in enumerate((first_ref, second_ref, third_ref)):
 
             @pl.when(source_ref[0] == number)
             def _(ref=ref):
-                copy = pltpu.make_async_copy(ref, rows_ref, arrived)
+                copy = pltpu.make_async_copy(ref, rows_ref, landed)
                 copy.start()
                 copy.wait()
 
@@ -210,7 +219,7 @@
     out_ref[...] = phi(dot(normed_ref[...], weight_ref[...])).astype(BF16)
 
 
-def similarity_kernel(me_ref, starts_ref, queries_ref, keys_ref, totals_ref, high_out, low_out, inverse_out):
+def similarity_kernel(me_ref, starts_ref, queries_ref, keys_ref, totals_ref, inverse_ref, scaled_ref, probe_out, mix_out, scale_out):
     rows = keys_ref.shape[0]
     me = me_ref[0]
     last = jnp.int32(-1)
@@ -218,57 +227,90 @@
         last = jnp.where(me == s, value, last)
     fresh = (last < 0).astype(F32)
     queries = queries_ref[...]
+    wide = queries.astype(F32)
     other = lax.broadcasted_iota(jnp.int32, (1, rows), 1) // MEM
     masked = jnp.where((other >= last) & (other < me), dot(queries, keys_ref[...], ((1,), (1,))), 0.0)
-    base = jnp.sum(queries.astype(F32) * totals_ref[...], axis=-1, keepdims=True)
+    base = jnp.sum(wide * totals_ref[...], axis=-1, keepdims=True)
     inverse = 1.0 / jnp.maximum(fresh * base + jnp.sum(masked, axis=-1, keepdims=True), 1.0)
-    high_out[...], low_out[...] = split(masked)
-    lane = lax.broadcasted_iota(jnp.int32, inverse_out.shape, 1)
-    inverse_out[...] = jnp.where(lane < 64, inverse, inverse * fresh)
-
-
-def read_kernel(place_ref, queries_ref, high_ref, low_ref, inverse_ref, rows_ref, matrix_ref, mine_ref, theirs_ref, *rest):
-    out_ref = rest[-1]
+    masked = masked.astype(BF16)
+    mix_out[...] = dot(masked, inverse_ref[...]).astype(BF16)
+    probed = dot(dot(masked, scaled_ref[...]).astype(BF16), keys_ref[...])
+    probe_out[...] = (fresh * wide - probed).astype(BF16)
+    scale_out[...] = jnp.broadcast_to(inverse, scale_out.shape)
+
+
+def near_copies(z, place_ref, held_ref, arrived, matrix_ref):
+    wide = held_ref.shape[1]
+    return [pltpu.make_async_copy(matrix_ref.at[pl.ds(z * wide, wide)], held_ref.at[z], arrived.at[z, 0])]
+
+
+def away_copies(z, place_ref, held_ref, arrived, matrix_ref, bulk_ref):
+    few = bulk_ref.shape[1]
+    width = held_ref.shape[1] // 2
+    many = width - few
+    return [
+        pltpu.make_async_copy(source, held_ref.at[z, pl.ds(start, size)], arrived.at[z, number])
+        for number, (source, start, size) in enumerate(
+            (
+                (matrix_ref.at[pl.ds(2 * z * many, many)], 0, many),
+                (bulk_ref.at[2 * z], many, few),
+                (matrix_ref.at[pl.ds((2 * z + 1) * many, many)], width, many),
+                (bulk_ref.at[2 * z + 1], width + many, few),
+            )
+        )
+    ]
+
+
+def read_kernel(copies, parts, place_ref, probe_ref, mix_ref, scale_ref, rows_ref, mine_ref, theirs_ref, *rest):
+    matrix_refs, (out_ref, held_ref, arrived) = rest[:parts], rest[-3:]
+    step = pl.program_id(0)
+
+    @pl.when(step == 0)
+    def _():
+        for z in range(4):
+            for copy in copies(z, place_ref, held_ref, arrived, *matrix_refs):
+                copy.start()
+
+    for copy in copies(step, place_ref, held_ref, arrived, *matrix_refs):
+        copy.wait()
     width = mine_ref.shape[2]
-    base = dot(queries_ref[...], matrix_ref[...], ((1,), (1,)))
-    inverse = inverse_ref[:, :1]
-    fresh = inverse_ref[:, 64:65]
+    base = dot(probe_ref[...], held_ref[step], ((1,), (1,)))
+    scale = scale_ref[:, :1]
     swap = place_ref[1] == 1
     for side in range(2):
         cols = slice(side * width, (side + 1) * width)
         writes = jnp.where(swap == (side == 0), theirs_ref[0], mine_ref[0])
-        low = dot(high_ref[...], writes) + dot(low_ref[...], writes)
-        out_ref[:, cols] = (rows_ref[:, cols].astype(F32) + (fresh * base[:, cols] + inverse * low)).astype(BF16)
-
-
-def read_half(half, me, queries, high, low, inverse, entering, matrix, writes, previous=None):
-    count, depth = queries.shape
-    rows, width = writes[0].shape[1:]
+        low = dot(mix_ref[...], writes)
+        out_ref[:, cols] = (rows_ref[:, cols].astype(F32) + scale * (base[:, cols] + low)).astype(BF16)
+
+
+def read_half(half, me, probe, mix, scale, entering, values, matrices, copies, previous=None):
+    count, depth = probe.shape
+    rows, width = values[0].shape[1:]
     distance = (jnp.arange(4, dtype=jnp.int32) - me // 4) % 4
     slot_of = jnp.where(distance == 3, 1, jnp.where(distance == 0, 0, distance + 1))
     place = jnp.concatenate([jnp.stack([half, me % 2]), slot_of])
-    args = [place, queries, high, low, inverse, entering, matrix, *writes]
+    args = [place, probe, mix, scale, entering, *values, *matrices]
     specs = [
         pl.BlockSpec((count, depth), lambda z, p: (0, 0)),
         pl.BlockSpec((count, rows), lambda z, p: (0, 0)),
-        pl.BlockSpec((count, rows), lambda z, p: (0, 0)),
         pl.BlockSpec((count, 128), lambda z, p: (0, 0)),
         pl.BlockSpec((count, 2 * width), lambda z, p: (0, 2 * z + p[0])),
-        pl.BlockSpec((2 * width, depth), lambda z, p: (z, 0)),
         pl.BlockSpec((1, rows, width), lambda z, p: (p[2 + z], 0, 0)),
         pl.BlockSpec((1, rows, width), lambda z, p: (p[2 + z], 0, 0)),
-    ]
+    ] + [pl.BlockSpec(memory_space=pl.ANY)] * len(matrices)
     if previous is not None:
         args.append(previous)
         specs.append(pl.BlockSpec(memory_space=pl.ANY))
     return pl.pallas_call(
-        read_kernel,
+        functools.partial(read_kernel, copies, len(matrices)),
         out_shape=shape(entering.shape, BF16),
         grid_spec=pltpu.PrefetchScalarGridSpec(
             num_scalar_prefetch=1,
             grid=(4,),
             in_specs=specs,
             out_specs=pl.BlockSpec((count, 2 * width), lambda z, p: (0, 2 * z + p[0])),
+            scratch_shapes=[pltpu.VMEM((4, 2 * width, depth), BF16), pltpu.SemaphoreType.DMA((4, 4))],
         ),
         input_output_aliases={} if previous is None else {len(args) - 1: 0},
         interpret=INTERPRET,
@@ -299,27 +341,35 @@
     entering = shifted_rows(leaving)
     groups = [[i for i in range(16) if (i // 2) % 2 == y] for y in (0, 1)]
     near = lax.all_gather(matrix, "seg", axis=0, tiled=True, axis_index_groups=groups)
-    partner = permute(matrix, "seg", lambda i: i ^ 2)
+    trimmed = matrix[: 7 * width // 8]
+    partner = permute(trimmed, "seg", lambda i: i ^ 2)
     away = lax.all_gather(partner, "seg", axis=0, tiled=True, axis_index_groups=groups)
+    bulk = near.reshape(8, width, depth)[:, 7 * width // 8 :]
+    bulk = permute(bulk, "seg", lambda i: i ^ 2)
 
     normed = call(
         norm_kernel, shape((2, MEM, features), BF16), head, across, norm_gain, specs=[VM] * 3
     )
     memory = gather_pairs(normed)
-    key_part, values, rates = call(
+    key_part, values, sent, rates = call(
         kv_kernel,
-        (shape((rows, w_key.shape[2]), BF16), shape((rows, width), F32), shape((rows, 128), F32)),
+        (
+            shape((rows, w_key.shape[2]), BF16),
+            shape((rows, width), F32),
+            shape((rows, width), BF16),
+            shape((rows, 128), F32),
+        ),
         pair_slots, *memory, w_key[0], w_value[0], w_gate,
         specs=[SM] + [VM] * 11,
     )
     pieces = gather_slots(key_part)
-    keys, writes, sent = call(
+    value_slots = gather_slots(sent)
+    keys, writes, inverse, scaled = call(
         solve_kernel,
-        (shape((rows, depth), BF16), shape((rows, width), F32), shape((rows, width), BF16)),
+        (shape((rows, depth), BF16), shape((rows, width), F32), shape((rows, rows), BF16), shape((rows, rows), BF16)),
         slots, doc_starts, *pieces, values, rates, matrix, key_totals,
         specs=[SM, SM] + [VM] * 8,
     )
-    write_slots = gather_slots(sent)
     matrix_next, totals_next = call(
         next_kernel,
         (shape((width, depth), BF16), shape((1, depth), F32)),
@@ -328,16 +378,15 @@
     )
 
     count = leaving.shape[0]
+    any_space = pl.BlockSpec(memory_space=pl.ANY)
     block = depth // 4
     queries, entering = pl.pallas_call(
         query_kernel,
         out_shape=(shape((count, depth), BF16), shape((count, features), BF16)),
         grid=(4,),
-        in_specs=[
-            SM,
-            pl.BlockSpec(memory_space=pl.ANY),
-            pl.BlockSpec(memory_space=pl.ANY),
-            pl.BlockSpec(memory_space=pl.ANY),
+        in_specs=[SM]
+        + [any_space] * 3
+        + [
             pl.BlockSpec((1, features), lambda j: (0, 0)),
             pl.BlockSpec((features, block), lambda j: (0, j)),
         ],
@@ -345,16 +394,20 @@
         scratch_shapes=[pltpu.VMEM((count, features), BF16), pltpu.SemaphoreType.DMA],
         interpret=INTERPRET,
     )(*entering, norm_gain, w_query[0])
-    high, low, inverse = call(
+    probe, mix, scale = call(
         similarity_kernel,
-        (shape((count, rows), BF16), shape((count, rows), BF16), shape((count, 128), F32)),
-        mine, doc_starts, queries, keys, key_totals,
-        specs=[SM, SM] + [VM] * 3,
+        (
+            shape((count, depth), BF16),
+            shape((count, rows), BF16),
+            shape((count, 128), F32),
+        ),
+        mine, doc_starts, queries, keys, key_totals, inverse, scaled,
+        specs=[SM, SM] + [VM] * 5,
     )
     half = (me // 2) % 2
-    parts = (me, queries, high, low, inverse, entering)
-    updated = read_half(half, *parts, near, write_slots[0::2])
-    updated = read_half(1 - half, *parts, away, write_slots[1::2], updated)
+    parts = (me, probe, mix, scale, entering)
+    updated = read_half(half, *parts, value_slots[0::2], (near,), near_copies)
+    updated = read_half(1 - half, *parts, value_slots[1::2], (away, bulk), away_copies, updated)
     return updated[None, None], matrix_next[None], totals_next
 
 

time: 198 us -> 235 us (1.19)
  waiting for transfers between devices: 79.1 us -> 119 us
  starting transfers between devices: 44.3 us -> 37.5 us
    ppermute x21 -> x22, waiting for transfers between devices: 75.1 us -> 115 us  [permute(): return lax.ppermute(block, axis, [(i, target(i)) for i in range(size)])]
    ppermute x21 -> x22, starting transfers between devices: 33.4 us -> 26.7 us  [permute(): return lax.ppermute(block, axis, [(i, target(i)) for i in range(size)])]
    slice x0 -> x2, local copies, waits for them, and re-layouts: none -> 3.66 us  [the longest x1 2.39 us: local(): bulk = near.reshape(8, width, depth)[:, 7 * width // 8:]]
  transfers between devices with their start and end apart: 28 -> 29, of which waited for: 12 -> 13; matrix products, arithmetic and copies ran while one was open for 3% -> 4% of each run, Pallas kernels for 21% -> 18%
where the time goes in v1:
time: 235 us; the launch traced here: 234 us
  waiting for transfers between devices  119 us (51%)
  Pallas kernels  50.8 us (22%)
  starting transfers between devices  37.5 us (16%)
  between operations  14.9 us (6%)
  local copies, waits for them, and re-layouts  6.95 us (3%)
  other arithmetic  4.71 us (2%)
    ppermute x22, waiting for transfers between devices, permute(): return lax.ppermute(block, axis, [(i, target(i)) for i in range(size)])  115 us
    ppermute x22, starting transfers between devices, permute(): return lax.ppermute(block, axis, [(i, target(i)) for i in range(size)])  26.7 us
    pallas_call x5, Pallas kernels, call(): pl.pallas_call(kernel, out_shape=outs, in_specs=list(specs), out_specs=ja...  19.9 us
    pallas_call x2, Pallas kernels, read_half(): pl.pallas_call(functools.partial(read_kernel, copies, len(matrices)), out...  17.4 us
    pallas_call x1, Pallas kernels, local(): pl.pallas_call(query_kernel, out_shape=(shape((count, depth), BF16), shap...  13.5 us
    ppermute x4, starting transfers between devices, send(): lax.ppermute(part, ('seg', 'section'), [(s * wide + p, s * wide + q) for...  8.81 us
  transfers between devices with their start and end apart: 29, of which 13 were waited for; matrix products, arithmetic and copies ran while one was open for 4% of the time, Pallas kernels for 18%

profile of v1, /device:TPU:1, one launch (start us, length us, event | category | flops | bytes accessed | tf_op | source)
XLA Modules:
  0.0 233.9 jit_solution(5315314922352411884)
XLA Ops:
  7.3 0.7 all-gather.6.cloned.1.call-update
  8.0 1.3 slice_bitcast_fusion
  9.3 2.2 collective-permute-start.24
  11.5 19.8 %collective-permute-done.24 = bf16[224,2048]{1,0:T(8,128)(2,1)S(1)} collective-permute-done((bf16[224,2048]{1,0:T(8,128)(2,1)S(1)}, bf16[224,2048]{1,0:T(8,128)(2,1)S(1)}, u32[]{:S(2)}, u32[]{:S(2)}) %collective-permute-start.24) | collective-permute-done | bytes 917536 | tf_op jit(solution)/shard_map/ppermute | solution.py:24
  31.3 0.9 copy-done.3
  32.2 2.1 collective-permute-start.2
  34.3 3.5 %collective-permute-start = (bf16[272,4096]{1,0:T(8,128)(2,1)}, bf16[272,4096]{1,0:T(8,128)(2,1)S(1)}, u32[]{:S(2)}, u32[]{:S(2)}) collective-permute-start(bf16[272,4096]{1,0:T(8,128)(2,1)} %bitcast.43), channel_id=1, source_target_pairs={{0,1},{1,2},{2,3},{4,5},{5,6},{6,7},{8,9},{9,10},{10,11},{12,13},{... | collective-permute-start | bytes 6684680 | tf_op jit(solution)/shard_map/ppermute | solution.py:48
  37.8 0.9 slice_bitcast_fusion.1
  38.7 1.2 collective-permute-start.4
  39.8 1.9 collective-permute-start.5
  41.8 45.2 %collective-permute-done.4.rows_ref = bf16[16,4096]{1,0:T(8,128)(2,1)S(1)} collective-permute-done((bf16[16,4096]{1,0:T(8,128)(2,1)S(1)}, bf16[16,4096]{1,0:T(8,128)(2,1)S(1)}, u32[]{:S(2)}, u32[]{:S(2)}) %collective-permute-start.4) | collective-permute-done | bytes 131104 | tf_op jit(solution)/shard_map/ppermute | solution.py:24
  87.0 2.8 %collective-permute-done.5.across_ref = bf16[16,4096]{1,0:T(8,128)(2,1)S(1)} collective-permute-done((bf16[16,4096]{1,0:T(8,128)(2,1)S(1)}, bf16[16,4096]{1,0:T(8,128)(2,1)S(1)}, u32[]{:S(2)}, u32[]{:S(2)}) %collective-permute-start.5) | collective-permute-done | bytes 131104 | tf_op jit(solution)/shard_map/ppermute | solution.py:38
  90.5 1.8 shard_map.176.refs_0_
  92.3 1.6 collective-permute-start.6
  93.9 2.2 collective-permute-start.7
  96.1 1.2 collective-permute-start.8
  97.4 10.9 %collective-permute-done.6.refs_1_ = bf16[2,16,4096]{2,1,0:T(8,128)(2,1)S(1)} collective-permute-done((bf16[2,16,4096]{2,1,0:T(8,128)(2,1)}, bf16[2,16,4096]{2,1,0:T(8,128)(2,1)S(1)}, u32[]{:S(2)}, u32[]{:S(2)}) %collective-permute-start.6) | collective-permute-done | bytes 262176 | tf_op jit(solution)/shard_map/ppermute | solution.py:24
  108.3 3.0 %collective-permute-start.9 = (bf16[2,16,4096]{2,1,0:T(8,128)(2,1)}, bf16[2,16,4096]{2,1,0:T(8,128)(2,1)S(1)}, u32[]{:S(2)}, u32[]{:S(2)}) collective-permute-start(bf16[2,16,4096]{2,1,0:T(8,128)(2,1)} %shard_map.176.refs_0_), channel_id=1, source_target_pairs={{0,8},{8,0},{16,24},{24,16},{32,40},{40,32},{48,56},{56,48},{64,72... | collective-permute-start | bytes 786440 | tf_op jit(solution)/shard_map/ppermute | solution.py:24
  111.5 7.6 %collective-permute-done.8.refs_3_ = bf16[2,16,4096]{2,1,0:T(8,128)(2,1)S(1)} collective-permute-done((bf16[2,16,4096]{2,1,0:T(8,128)(2,1)}, bf16[2,16,4096]{2,1,0:T(8,128)(2,1)S(1)}, u32[]{:S(2)}, u32[]{:S(2)}) %collective-permute-start.8) | collective-permute-done | bytes 262176 | tf_op jit(solution)/shard_map/ppermute | solution.py:24
  119.2 2.0 collective-permute-start.1
  121.2 1.3 collective-permute-start.3
  122.5 1.3 collective-permute-start.11
  123.9 1.3 xor_add_fusion
  125.5 5.2 %shard_map.177 = (bf16[256,128]{1,0:T(8,128)(2,1)}, f32[256,256]{1,0:T(8,128)}, bf16[256,256]{1,0:T(8,128)(2,1)}, f32[256,128]{1,0:T(8,128)}) custom-call(s32[16]{0:T(128)} %get-tuple-element.35.slots_ref, bf16[2,16,4096]{2,1,0:T(8,128)(2,1)} %shard_map.176.refs_0_, bf16[2,16,4096]{2,1,0:T(8,128)(2,1)} %copy-done.6, bf16[2,16,4096]{2,1,0:T(8,128)(2,1)} %copy-done.7, ...), custom_call_target="tpu_custom_call" | custom-call | tf_op jit(solution)/shard_map/pallas_call | solution.py:321
  130.6 1.0 collective-permute-start.13
  131.6 1.8 collective-permute-start.14
  133.4 2.3 collective-permute-done.13
  136.4 4.5 %collective-permute-done.15 = bf16[256,128]{1,0:T(8,128)(2,1)S(1)} collective-permute-done((bf16[256,128]{1,0:T(8,128)(2,1)}, bf16[256,128]{1,0:T(8,128)(2,1)S(1)}, u32[]{:S(2)}, u32[]{:S(2)}) %collective-permute-start.15) | collective-permute-done | bytes 65568 | tf_op jit(solution)/shard_map/ppermute | solution.py:24
  141.0 0.9 pad_maximum_fusion.1.a_ref
  141.9 1.5 collective-permute-done.19
  143.4 1.3 collective-permute-start.16
  145.5 5.8 %collective-permute-done.21 = bf16[256,256]{1,0:T(8,128)(2,1)S(1)} collective-permute-done((bf16[256,256]{1,0:T(8,128)(2,1)}, bf16[256,256]{1,0:T(8,128)(2,1)S(1)}, u32[]{:S(2)}, u32[]{:S(2)}) %collective-permute-start.21) | collective-permute-done | bytes 131104 | tf_op jit(solution)/shard_map/ppermute | solution.py:24
  151.2 4.1 %collective-permute-start.17 = (bf16[4,256,128]{2,1,0:T(8,128)(2,1)S(1)}, bf16[4,256,128]{2,1,0:T(8,128)(2,1)S(1)}, u32[]{:S(2)}, u32[]{:S(2)}) collective-permute-start(bf16[4,256,128]{2,1,0:T(8,128)(2,1)S(1)} %pad_maximum_fusion.1.a_ref), channel_id=1, source_target_pairs={{0,8},{8,0},{16,24},{24,16},{32,40},{40,32},{48,56},{56,48},{64,72... | collective-permute-start | bytes 786440 | tf_op jit(solution)/shard_map/ppermute | solution.py:24
  155.8 2.0 collective-permute-start.18
  157.8 1.0 pad_maximum_fusion.mine_ref
  158.8 0.7 copy-done.5
  159.6 1.3 collective-permute-start.22
  160.8 2.4 %slice.21 = bf16[8,32,2048]{2,1,0:T(8,128)(2,1)} slice(bf16[8,256,2048]{2,1,0:T(8,128)(2,1)} %bitcast.29), slice={[0:8], [224:256], [0:2048]} | slice | bytes 2097152 | tf_op jit(solution)/shard_map/slice | solution.py:347
  163.4 16.3 %collective-permute-done.22.mine_ref = bf16[4,256,256]{2,1,0:T(8,128)(2,1)S(1)} collective-permute-done((bf16[4,256,256]{2,1,0:T(8,128)(2,1)S(1)}, bf16[4,256,256]{2,1,0:T(8,128)(2,1)S(1)}, u32[]{:S(2)}, u32[]{:S(2)}) %collective-permute-start.22) | collective-permute-done | bytes 524320 | tf_op jit(solution)/shard_map/ppermute | solution.py:24
  179.7 0.9 collective-permute-start.26
  180.8 0.9 compare_reduce_fusion
  182.4 0.7 add_add_fusion.1
  183.1 5.6 %shard_map.178 = (bf16[256,2048]{1,0:T(8,128)(2,1)}, f32[256,256]{1,0:T(8,128)}, bf16[256,256]{1,0:T(8,128)(2,1)}, bf16[256,256]{1,0:T(8,128)(2,1)}) custom-call(s32[16]{0:T(128)} %get-tuple-element.36.slots_ref, s32[1,16]{1,0:T(1,128)} %starts_ref.5, bf16[4,256,128]{2,1,0:T(8,128)(2,1)} %copy-done.2, bf16[4,256,128]{2,1,0:T(8,128)(2,1)} %collective-permute-done.16.b_ref, ...), custom_call_target="tpu_custom_call" | custom-call | tf_op jit(solution)/shard_map/pallas_call | solution.py:321
  188.7 3.1 %shard_map.182 = (bf16[256,2048]{1,0:T(8,128)(2,1)}, f32[1,2048]{1,0:T(1,128)}) custom-call(s32[1,16]{1,0:T(1,128)} %starts_ref.5, bf16[256,2048]{1,0:T(8,128)(2,1)} %get-tuple-element.22.keys_ref, f32[256,256]{1,0:T(8,128)} %get-tuple-element.30.writes_ref, bf16[256,2048]{1,0:T(8,128)(2,1)} %bitcast.28, f32[1,2048]{1,0:T(1,128)} %totals_ref.5), custom_call_target="tpu_custom_call" | custom-call | tf_op jit(solution)/shard_map/pallas_call | solution.py:321
  191.8 13.5 %shard_map.175 = (bf16[272,2048]{1,0:T(8,128)(2,1)}, bf16[272,4096]{1,0:T(8,128)(2,1)}) custom-call(s32[1]{0:T(128)} %bitcast.3.source_ref, bf16[272,4096]{1,0:T(8,128)(2,1)} %copy-done, bf16[272,4096]{1,0:T(8,128)(2,1)} %collective-permute-done.1.second_ref, bf16[272,4096]{1,0:T(8,128)(2,1)} %collective-permute-done.3.third_ref, bf16[1,4096]{1,0:T(2,128)(2,1)} %gain_ref.3, ...), custom_call_target="tpu_custom_call" | custom-call | tf_op jit(solution)/shard_map/pallas_call | solution.py:383
  205.3 4.2 %shard_map.179 = (bf16[272,2048]{1,0:T(8,128)(2,1)}, bf16[272,256]{1,0:T(8,128)(2,1)}, f32[272,128]{1,0:T(8,128)}) custom-call(s32[1]{0:T(128)} %bitcast.2.me_ref, s32[1,16]{1,0:T(1,128)} %starts_ref.5, bf16[272,2048]{1,0:T(8,128)(2,1)} %get-tuple-element.18.queries_ref, bf16[256,2048]{1,0:T(8,128)(2,1)} %get-tuple-element.22.keys_ref, ...), custom_call_target="tpu_custom_call" | custom-call | tf_op jit(solution)/shard_map/pallas_call | solution.py:321
  209.6 8.7 %shard_map.180.rest_2_ = bf16[272,4096]{1,0:T(8,128)(2,1)} custom-call(s32[6]{0:T(128)} %get-tuple-element.33.place_ref, bf16[272,2048]{1,0:T(8,128)(2,1)} %get-tuple-element.25.probe_ref, bf16[272,256]{1,0:T(8,128)(2,1)} %get-tuple-element.26.mix_ref, f32[272,128]{1,0:T(8,128)} %get-tuple-element.27.scale_ref, ...), custom_call_target="tpu_custom_call" | custom-call | tf_op jit(solution)/shard_map/pallas_call | solution.py:305
  218.3 8.7 %shard_map.181 = bf16[272,4096]{1,0:T(8,128)(2,1)} custom-call(s32[6]{0:T(128)} %get-tuple-element.34.place_ref, bf16[272,2048]{1,0:T(8,128)(2,1)} %get-tuple-element.25.probe_ref, bf16[272,256]{1,0:T(8,128)(2,1)} %get-tuple-element.26.mix_ref, f32[272,128]{1,0:T(8,128)} %get-tuple-element.27.scale_ref, ...), custom_call_target="tpu_custom_call", output_to_operand_aliasing={{}: (9, {})} | custom-call | tf_op jit(solution)/shard_map/pallas_call | solution.py:305
  (65 shorter events, 4.2 us)
Async XLA Ops:
  7.2 116.7 %copy-start.13 = (s32[16]{0:T(128)S(1)}, s32[16]{0:T(128)}, u32[]{:S(2)}) copy-start(s32[16]{0:T(128)} %constant.121.clone) | copy-start | bytes 196
  7.2 116.7 %copy-start.14 = (s32[16]{0:T(128)S(1)}, s32[16]{0:T(128)}, u32[]{:S(2)}) copy-start(s32[16]{0:T(128)} %constant.122.clone) | copy-start | bytes 196
  7.2 116.7 %copy-start.15 = (s32[16]{0:T(128)S(1)}, s32[16]{0:T(128)}, u32[]{:S(2)}) copy-start(s32[16]{0:T(128)} %constant.123.clone) | copy-start | bytes 196
  7.2 116.7 %copy-start.16 = (s32[16]{0:T(128)S(1)}, s32[16]{0:T(128)}, u32[]{:S(2)}) copy-start(s32[16]{0:T(128)} %constant.124.clone) | copy-start | bytes 196
  7.2 153.6 %all-gather.6.cloned.1.call-start = ((), (), s32[]{:S(2)}) async-start(), calls=%async_computation.1 | async-start | bytes 9437184 | tf_op jit(solution)/shard_map/all_gather | solution.py:343
  7.9 210.3 %all-gather.4.cloned.1.call-start = ((), (), s32[]{:S(2)}) async-start(), calls=%async_computation | async-start | bytes 8257536 | tf_op jit(solution)/shard_map/all_gather | solution.py:346
  9.3 22.0 %collective-permute-start.24 = (bf16[224,2048]{1,0:T(8,128)(2,1)S(1)}, bf16[224,2048]{1,0:T(8,128)(2,1)S(1)}, u32[]{:S(2)}, u32[]{:S(2)}) collective-permute-start(bf16[224,2048]{1,0:T(8,128)(2,1)S(1)} %slice_bitcast_fusion), channel_id=1, source_target_pairs={{0,16},{8,24},{16,0},{24,8},{32,48},{40,56},{48,32},{56,40},{64,80... | collective-permute-start | bytes 2752520 | tf_op jit(solution)/shard_map/ppermute | solution.py:24
  31.3 0.9 copy-start.3
  32.2 88.9 %collective-permute-start.2 = (bf16[272,4096]{1,0:T(8,128)(2,1)}, bf16[272,4096]{1,0:T(8,128)(2,1)}, u32[]{:S(2)}, u32[]{:S(2)}) collective-permute-start(bf16[272,4096]{1,0:T(8,128)(2,1)} %bitcast.42), channel_id=1, source_target_pairs={{11,15},{15,11},{19,23},{23,19},{43,47},{47,43},{51,55},{55,51},{7... | collective-permute-start | bytes 6684680 | tf_op jit(solution)/shard_map/ppermute | solution.py:48
  34.3 146.3 %collective-permute-start = (bf16[272,4096]{1,0:T(8,128)(2,1)}, bf16[272,4096]{1,0:T(8,128)(2,1)S(1)}, u32[]{:S(2)}, u32[]{:S(2)}) collective-permute-start(bf16[272,4096]{1,0:T(8,128)(2,1)} %bitcast.43), channel_id=1, source_target_pairs={{0,1},{1,2},{2,3},{4,5},{5,6},{6,7},{8,9},{9,10},{10,11},{12,13},{... | collective-permute-start | bytes 6684680 | tf_op jit(solution)/shard_map/ppermute | solution.py:48
  38.7 48.3 %collective-permute-start.4 = (bf16[16,4096]{1,0:T(8,128)(2,1)S(1)}, bf16[16,4096]{1,0:T(8,128)(2,1)S(1)}, u32[]{:S(2)}, u32[]{:S(2)}) collective-permute-start(bf16[16,4096]{1,0:T(8,128)(2,1)S(1)} %slice_bitcast_fusion.1), channel_id=1, source_target_pairs={{0,1},{1,2},{2,3},{3,4},{4,5},{5,6},{6,7},{7,0},{8,9},{9,10},{10,1... | collective-permute-start | bytes 393224 | tf_op jit(solution)/shard_map/ppermute | solution.py:24
  39.8 50.0 %collective-permute-start.5 = (bf16[16,4096]{1,0:T(8,128)(2,1)S(1)}, bf16[16,4096]{1,0:T(8,128)(2,1)S(1)}, u32[]{:S(2)}, u32[]{:S(2)}) collective-permute-start(bf16[16,4096]{1,0:T(8,128)(2,1)S(1)} %slice_bitcast_fusion.1), channel_id=1, source_target_pairs={{0,17},{1,18},{2,19},{3,20},{4,21},{5,22},{6,23},{7,16},{8,25},{9,... | collective-permute-start | bytes 393224 | tf_op jit(solution)/shard_map/ppermute | solution.py:38
  87.0 2.8 %copy-start.11 = (bf16[16,4096]{1,0:T(8,128)(2,1)}, bf16[16,4096]{1,0:T(8,128)(2,1)S(1)}, u32[]{:S(2)}) copy-start(bf16[16,4096]{1,0:T(8,128)(2,1)S(1)} %collective-permute-done.4.rows_ref) | copy-start | bytes 393220
  89.8 0.6 copy-start.12
  92.3 16.0 %collective-permute-start.6 = (bf16[2,16,4096]{2,1,0:T(8,128)(2,1)}, bf16[2,16,4096]{2,1,0:T(8,128)(2,1)S(1)}, u32[]{:S(2)}, u32[]{:S(2)}) collective-permute-start(bf16[2,16,4096]{2,1,0:T(8,128)(2,1)} %shard_map.176.refs_0_), channel_id=1, source_target_pairs={{0,32},{8,40},{16,48},{24,56},{32,64},{40,72},{48,80},{56,88},{64,... | collective-permute-start | bytes 786440 | tf_op jit(solution)/shard_map/ppermute | solution.py:24
  93.9 17.3 %collective-permute-start.7 = (bf16[2,16,4096]{2,1,0:T(8,128)(2,1)}, bf16[2,16,4096]{2,1,0:T(8,128)(2,1)S(1)}, u32[]{:S(2)}, u32[]{:S(2)}) collective-permute-start(bf16[2,16,4096]{2,1,0:T(8,128)(2,1)} %shard_map.176.refs_0_), channel_id=1, source_target_pairs={{0,96},{8,104},{16,112},{24,120},{32,0},{40,8},{48,16},{56,24},{64... | collective-permute-start | bytes 786440 | tf_op jit(solution)/shard_map/ppermute | solution.py:24
  96.1 23.0 %collective-permute-start.8 = (bf16[2,16,4096]{2,1,0:T(8,128)(2,1)}, bf16[2,16,4096]{2,1,0:T(8,128)(2,1)S(1)}, u32[]{:S(2)}, u32[]{:S(2)}) collective-permute-start(bf16[2,16,4096]{2,1,0:T(8,128)(2,1)} %shard_map.176.refs_0_), channel_id=1, source_target_pairs={{0,64},{8,72},{16,80},{24,88},{32,96},{40,104},{48,112},{56,120},{... | collective-permute-start | bytes 786440 | tf_op jit(solution)/shard_map/ppermute | solution.py:24
  108.3 17.2 %copy-start.6 = (bf16[2,16,4096]{2,1,0:T(8,128)(2,1)}, bf16[2,16,4096]{2,1,0:T(8,128)(2,1)S(1)}, u32[]{:S(2)}) copy-start(bf16[2,16,4096]{2,1,0:T(8,128)(2,1)S(1)} %collective-permute-done.6.refs_1_) | copy-start | bytes 786436
  108.3 14.2 %collective-permute-start.9 = (bf16[2,16,4096]{2,1,0:T(8,128)(2,1)}, bf16[2,16,4096]{2,1,0:T(8,128)(2,1)S(1)}, u32[]{:S(2)}, u32[]{:S(2)}) collective-permute-start(bf16[2,16,4096]{2,1,0:T(8,128)(2,1)} %shard_map.176.refs_0_), channel_id=1, source_target_pairs={{0,8},{8,0},{16,24},{24,16},{32,40},{40,32},{48,56},{56,48},{64,72... | collective-permute-start | bytes 786440 | tf_op jit(solution)/shard_map/ppermute | solution.py:24
  111.3 14.2 %copy-start.7 = (bf16[2,16,4096]{2,1,0:T(8,128)(2,1)}, bf16[2,16,4096]{2,1,0:T(8,128)(2,1)S(1)}, u32[]{:S(2)}) copy-start(bf16[2,16,4096]{2,1,0:T(8,128)(2,1)S(1)} %collective-permute-done.7.refs_2_) | copy-start | bytes 786436
  111.3 12.5 %collective-permute-start.10 = (bf16[2,16,4096]{2,1,0:T(8,128)(2,1)S(1)}, bf16[2,16,4096]{2,1,0:T(8,128)(2,1)S(1)}, u32[]{:S(2)}, u32[]{:S(2)}) collective-permute-start(bf16[2,16,4096]{2,1,0:T(8,128)(2,1)S(1)} %collective-permute-done.6.refs_1_), channel_id=1, source_target_pairs={{0,8},{8,0},{16,24},{24,16},{32,40},{40,32},{48,56},{56,48},{64,72... | collective-permute-start | bytes 786440 | tf_op jit(solution)/shard_map/ppermute | solution.py:24
  119.2 6.3 %copy-start.8 = (bf16[2,16,4096]{2,1,0:T(8,128)(2,1)}, bf16[2,16,4096]{2,1,0:T(8,128)(2,1)S(1)}, u32[]{:S(2)}) copy-start(bf16[2,16,4096]{2,1,0:T(8,128)(2,1)S(1)} %collective-permute-done.8.refs_3_) | copy-start | bytes 786436
  119.2 72.7 %collective-permute-start.1 = (bf16[272,4096]{1,0:T(8,128)(2,1)}, bf16[272,4096]{1,0:T(8,128)(2,1)}, u32[]{:S(2)}, u32[]{:S(2)}) collective-permute-start(bf16[272,4096]{1,0:T(8,128)(2,1)} %bitcast.44), channel_id=1, source_target_pairs={{3,4},{7,0},{27,28},{31,24},{35,36},{39,32},{59,60},{63,56},{67,68... | collective-permute-start | bytes 6684680 | tf_op jit(solution)/shard_map/ppermute | solution.py:48
  121.2 70.7 %collective-permute-start.3 = (bf16[272,4096]{1,0:T(8,128)(2,1)}, bf16[272,4096]{1,0:T(8,128)(2,1)}, u32[]{:S(2)}, u32[]{:S(2)}) collective-permute-start(bf16[272,4096]{1,0:T(8,128)(2,1)} %collective-permute-done.2), channel_id=1, source_target_pairs={{11,8},{15,12},{19,16},{23,20},{43,40},{47,44},{51,48},{55,52},{75... | collective-permute-start | bytes 6684680 | tf_op jit(solution)/shard_map/ppermute | solution.py:48
  122.5 3.0 %copy-start.9 = (bf16[2,16,4096]{2,1,0:T(8,128)(2,1)}, bf16[2,16,4096]{2,1,0:T(8,128)(2,1)S(1)}, u32[]{:S(2)}) copy-start(bf16[2,16,4096]{2,1,0:T(8,128)(2,1)S(1)} %collective-permute-done.9.refs_4_) | copy-start | bytes 786436
  122.5 2.7 %collective-permute-start.11 = (bf16[2,16,4096]{2,1,0:T(8,128)(2,1)S(1)}, bf16[2,16,4096]{2,1,0:T(8,128)(2,1)}, u32[]{:S(2)}, u32[]{:S(2)}) collective-permute-start(bf16[2,16,4096]{2,1,0:T(8,128)(2,1)S(1)} %collective-permute-done.7.refs_2_), channel_id=1, source_target_pairs={{0,8},{8,0},{16,24},{24,16},{32,40},{40,32},{48,56},{56,48},{64,72... | collective-permute-start | bytes 786440 | tf_op jit(solution)/shard_map/ppermute | solution.py:24
  123.8 1.7 copy-start.10
  123.8 1.7 collective-permute-start.12
  130.6 50.2 %copy-start.17 = (s32[8]{0:T(128)S(1)}, s32[8]{0:T(128)}, u32[]{:S(2)}) copy-start(s32[8]{0:T(128)} %constant.126.clone) | copy-start | bytes 100
  130.6 5.0 %collective-permute-start.13 = (bf16[256,128]{1,0:T(8,128)(2,1)}, bf16[256,128]{1,0:T(8,128)(2,1)S(1)}, u32[]{:S(2)}, u32[]{:S(2)}) collective-permute-start(bf16[256,128]{1,0:T(8,128)(2,1)} %get-tuple-element.19), channel_id=1, source_target_pairs={{0,32},{8,40},{16,48},{24,56},{32,64},{40,72},{48,80},{56,88},{64,... | collective-permute-start | bytes 196616 | tf_op jit(solution)/shard_map/ppermute | solution.py:24
  131.6 4.2 %collective-permute-start.14 = (bf16[256,128]{1,0:T(8,128)(2,1)}, bf16[256,128]{1,0:T(8,128)(2,1)S(1)}, u32[]{:S(2)}, u32[]{:S(2)}) collective-permute-start(bf16[256,128]{1,0:T(8,128)(2,1)} %get-tuple-element.19), channel_id=1, source_target_pairs={{0,96},{8,104},{16,112},{24,120},{32,0},{40,8},{48,16},{56,24},{64... | collective-permute-start | bytes 196616 | tf_op jit(solution)/shard_map/ppermute | solution.py:24
  135.6 5.2 %collective-permute-start.15 = (bf16[256,128]{1,0:T(8,128)(2,1)}, bf16[256,128]{1,0:T(8,128)(2,1)S(1)}, u32[]{:S(2)}, u32[]{:S(2)}) collective-permute-start(bf16[256,128]{1,0:T(8,128)(2,1)} %get-tuple-element.19), channel_id=1, source_target_pairs={{0,64},{8,72},{16,80},{24,88},{32,96},{40,104},{48,112},{56,120},{... | collective-permute-start | bytes 196616 | tf_op jit(solution)/shard_map/ppermute | solution.py:24
  135.8 7.6 %collective-permute-start.19 = (bf16[256,256]{1,0:T(8,128)(2,1)}, bf16[256,256]{1,0:T(8,128)(2,1)S(1)}, u32[]{:S(2)}, u32[]{:S(2)}) collective-permute-start(bf16[256,256]{1,0:T(8,128)(2,1)} %get-tuple-element.29), channel_id=1, source_target_pairs={{0,32},{8,40},{16,48},{24,56},{32,64},{40,72},{48,80},{56,88},{64,... | collective-permute-start | bytes 393224 | tf_op jit(solution)/shard_map/ppermute | solution.py:24
  140.9 4.4 %collective-permute-start.20 = (bf16[256,256]{1,0:T(8,128)(2,1)}, bf16[256,256]{1,0:T(8,128)(2,1)S(1)}, u32[]{:S(2)}, u32[]{:S(2)}) collective-permute-start(bf16[256,256]{1,0:T(8,128)(2,1)} %get-tuple-element.29), channel_id=1, source_target_pairs={{0,96},{8,104},{16,112},{24,120},{32,0},{40,8},{48,16},{56,24},{64... | collective-permute-start | bytes 393224 | tf_op jit(solution)/shard_map/ppermute | solution.py:24
  141.9 41.2 %copy-start.2 = (bf16[4,256,128]{2,1,0:T(8,128)(2,1)}, bf16[4,256,128]{2,1,0:T(8,128)(2,1)S(1)}, u32[]{:S(2)}) copy-start(bf16[4,256,128]{2,1,0:T(8,128)(2,1)S(1)} %pad_maximum_fusion.1.a_ref) | copy-start | bytes 786436
  143.4 12.4 %collective-permute-start.16 = (bf16[4,256,128]{2,1,0:T(8,128)(2,1)S(1)}, bf16[4,256,128]{2,1,0:T(8,128)(2,1)}, u32[]{:S(2)}, u32[]{:S(2)}) collective-permute-start(bf16[4,256,128]{2,1,0:T(8,128)(2,1)S(1)} %pad_maximum_fusion.1.a_ref), channel_id=1, source_target_pairs={{0,16},{8,24},{16,0},{24,8},{32,48},{40,56},{48,32},{56,40},{64,80... | collective-permute-start | bytes 786440 | tf_op jit(solution)/shard_map/ppermute | solution.py:24
  145.3 5.9 %collective-permute-start.21 = (bf16[256,256]{1,0:T(8,128)(2,1)}, bf16[256,256]{1,0:T(8,128)(2,1)S(1)}, u32[]{:S(2)}, u32[]{:S(2)}) collective-permute-start(bf16[256,256]{1,0:T(8,128)(2,1)} %get-tuple-element.29), channel_id=1, source_target_pairs={{0,64},{8,72},{16,80},{24,88},{32,96},{40,104},{48,112},{56,120},{... | collective-permute-start | bytes 393224 | tf_op jit(solution)/shard_map/ppermute | solution.py:24
  151.2 7.6 %collective-permute-start.17 = (bf16[4,256,128]{2,1,0:T(8,128)(2,1)S(1)}, bf16[4,256,128]{2,1,0:T(8,128)(2,1)S(1)}, u32[]{:S(2)}, u32[]{:S(2)}) collective-permute-start(bf16[4,256,128]{2,1,0:T(8,128)(2,1)S(1)} %pad_maximum_fusion.1.a_ref), channel_id=1, source_target_pairs={{0,8},{8,0},{16,24},{24,16},{32,40},{40,32},{48,56},{56,48},{64,72... | collective-permute-start | bytes 786440 | tf_op jit(solution)/shard_map/ppermute | solution.py:24
  155.8 7.4 %collective-permute-start.18 = (bf16[4,256,128]{2,1,0:T(8,128)(2,1)}, bf16[4,256,128]{2,1,0:T(8,128)(2,1)}, u32[]{:S(2)}, u32[]{:S(2)}) collective-permute-start(bf16[4,256,128]{2,1,0:T(8,128)(2,1)} %collective-permute-done.16.b_ref), channel_id=1, source_target_pairs={{0,8},{8,0},{16,24},{24,16},{32,40},{40,32},{48,56},{56,48},{64,72... | collective-permute-start | bytes 786440 | tf_op jit(solution)/shard_map/ppermute | solution.py:24
  158.8 29.9 %copy-start.1 = (bf16[4,256,256]{2,1,0:T(8,128)(2,1)}, bf16[4,256,256]{2,1,0:T(8,128)(2,1)S(1)}, u32[]{:S(2)}) copy-start(bf16[4,256,256]{2,1,0:T(8,128)(2,1)S(1)} %pad_maximum_fusion.mine_ref) | copy-start | bytes 1572868
  158.8 0.7 copy-start.5
  159.6 20.1 %collective-permute-start.22 = (bf16[4,256,256]{2,1,0:T(8,128)(2,1)S(1)}, bf16[4,256,256]{2,1,0:T(8,128)(2,1)S(1)}, u32[]{:S(2)}, u32[]{:S(2)}) collective-permute-start(bf16[4,256,256]{2,1,0:T(8,128)(2,1)S(1)} %pad_maximum_fusion.mine_ref), channel_id=1, source_target_pairs={{0,16},{8,24},{16,0},{24,8},{32,48},{40,56},{48,32},{56,40},{64,80... | collective-permute-start | bytes 1572872 | tf_op jit(solution)/shard_map/ppermute | solution.py:24
  163.2 55.1 %collective-permute-start.25 = (bf16[8,32,2048]{2,1,0:T(8,128)(2,1)}, bf16[8,32,2048]{2,1,0:T(8,128)(2,1)}, u32[]{:S(2)}, u32[]{:S(2)}) collective-permute-start(bf16[8,32,2048]{2,1,0:T(8,128)(2,1)} %slice.21), channel_id=1, source_target_pairs={{0,16},{8,24},{16,0},{24,8},{32,48},{40,56},{48,32},{56,40},{64,80... | collective-permute-start | bytes 3145736 | tf_op jit(solution)/shard_map/ppermute | solution.py:24
  179.7 12.1 %copy-start.4 = (bf16[4,256,256]{2,1,0:T(8,128)(2,1)}, bf16[4,256,256]{2,1,0:T(8,128)(2,1)S(1)}, u32[]{:S(2)}) copy-start(bf16[4,256,256]{2,1,0:T(8,128)(2,1)S(1)} %collective-permute-done.22.mine_ref) | copy-start | bytes 1572868
  179.7 29.8 %collective-permute-start.26 = (bf16[4,256,256]{2,1,0:T(8,128)(2,1)S(1)}, bf16[4,256,256]{2,1,0:T(8,128)(2,1)}, u32[]{:S(2)}, u32[]{:S(2)}) collective-permute-start(bf16[4,256,256]{2,1,0:T(8,128)(2,1)S(1)} %pad_maximum_fusion.mine_ref), channel_id=1, source_target_pairs={{0,8},{8,0},{16,24},{24,16},{32,40},{40,32},{48,56},{56,48},{64,72... | collective-permute-start | bytes 1572872 | tf_op jit(solution)/shard_map/ppermute | solution.py:24
  180.6 11.3 %copy-start = (bf16[272,4096]{1,0:T(8,128)(2,1)}, bf16[272,4096]{1,0:T(8,128)(2,1)S(1)}, u32[]{:S(2)}) copy-start(bf16[272,4096]{1,0:T(8,128)(2,1)S(1)} %collective-permute-done.first_ref) | copy-start | bytes 6684676
  180.6 37.7 %collective-permute-start.23 = (bf16[4,256,256]{2,1,0:T(8,128)(2,1)S(1)}, bf16[4,256,256]{2,1,0:T(8,128)(2,1)}, u32[]{:S(2)}, u32[]{:S(2)}) collective-permute-start(bf16[4,256,256]{2,1,0:T(8,128)(2,1)S(1)} %collective-permute-done.22.mine_ref), channel_id=1, source_target_pairs={{0,8},{8,0},{16,24},{24,16},{32,40},{40,32},{48,56},{56,48},{64,72... | collective-permute-start | bytes 1572872 | tf_op jit(solution)/shard_map/ppermute | solution.py:24
Sparse Core Ops, SparseCore 0:
  9.7 53.4 all-gather.5
  64.9 54.4 all-gather.3

commit v2 on v1

--- a/solution.py
+++ b/solution.py
@@ -51,10 +51,8 @@
     first = send(block, [(s, p, (p + 1) % wide) for s in segs if s not in late for p in ends])
     second = send(block, [(s, p, (p + run) % wide) for s in late for p in ends])
     second = send(second, [(s, p, p + 1 - run) for s in late for p in ends])
-    source = jnp.where(
-        lax.axis_index("section") % run > 0, 0,
-        jnp.where(jnp.isin(lax.axis_index("seg"), jnp.array(late)), 2, 1),
-    )
+    me = lax.axis_index("seg")
+    source = jnp.where(lax.axis_index("section") % run > 0, 0, 1 + (me + me // 2) % 2)
     return source.astype(jnp.int32)[None], plain, first, second
 
 
@@ -89,10 +87,10 @@
     return [(dz, dy, dc) for dc in (0, 1) for dz in (0, 3, 1, 2) for dy in (0, 1)]
 
 
-def slot_segments(me, order):
+def slot_segment(me, offset):
     z, y, c = me // 4, (me // 2) % 2, me % 2
-    dz, dy, dc = (jnp.array(v, jnp.int32) for v in zip(*order))
-    return ((z + dz) % 4) * 4 + (y ^ dy) * 2 + (c ^ dc)
+    dz, dy, dc = offset
+    return ((z + dz) % 4) * 4 + ((y + dy) % 2) * 2 + (c + dc) % 2
 
 
 def split(x):
@@ -133,7 +131,7 @@
     out_ref[1] = normalise(across_ref[...], gain_ref[...])
 
 
-def kv_kernel(slots_ref, *refs):
+def kv_kernel(me_ref, *refs):
     pairs, (key_ref, value_ref, gate_ref, key_out, value_out, sent_out, gate_out) = refs[:8], refs[8:]
     count = 16
     memory = jnp.concatenate([ref[...] for ref in pairs], axis=0)
@@ -144,8 +142,8 @@
     rates = jax.nn.sigmoid(dot(memory, gate, ((1,), (1,))))[:, :1]
     values = rates * values
     rates = jnp.broadcast_to(rates, (count * MEM, 128))
-    for slot in range(count):
-        rows = pl.ds(pl.multiple_of(slots_ref[slot] * MEM, MEM), MEM)
+    for slot, offset in enumerate(pair_offsets()):
+        rows = pl.ds(pl.multiple_of(slot_segment(me_ref[0], offset) * MEM, MEM), MEM)
         part = slice(slot * MEM, (slot + 1) * MEM)
         key_out[rows, :] = keys[part]
         value_out[rows, :] = values[part]
@@ -153,12 +151,12 @@
         gate_out[rows, :] = rates[part]
 
 
-def solve_kernel(slots_ref, starts_ref, a_ref, b_ref, c_ref, d_ref, values_ref, rates_ref, matrix_ref, totals_ref, keys_out, writes_out, inverse_out, scaled_out):
+def solve_kernel(me_ref, starts_ref, a_ref, b_ref, c_ref, d_ref, values_ref, rates_ref, matrix_ref, totals_ref, keys_out, writes_out, inverse_out, scaled_out):
     pieces = (a_ref, b_ref, c_ref, d_ref)
     each, rows, width = a_ref.shape
     count = 4 * each
-    for slot in range(count):
-        cols = pl.ds(pl.multiple_of(slots_ref[slot] * width, width), width)
+    for slot, offset in enumerate(offsets()):
+        cols = pl.ds(pl.multiple_of(slot_segment(me_ref[0], offset) * width, width), width)
         keys_out[:, cols] = pieces[slot // each][slot % each]
     keys = keys_out[...]
     gram = dot(keys, keys, ((1,), (1,)))
@@ -175,18 +173,17 @@
     rates = rates_ref[:, :1]
     weights = fresh * rates / scales
     same = lax.broadcasted_iota(jnp.int32, (rows, rows), 0) == lax.broadcasted_iota(jnp.int32, (rows, rows), 1)
-    current = jnp.concatenate(
-        [values_ref[...] - weights * probed, same.astype(F32), jnp.where(same, weights, 0.0)], axis=1
-    )
+    current = jnp.concatenate([values_ref[...] - weights * probed, same.astype(F32)], axis=1)
     power = split(masked * (rates / scales))
     current = current - dot3(power, split(current))
     for _ in range(3):
         power = split(dot3(power, power))
         current = current + dot3(power, split(current))
-    wide = current.shape[1] - 2 * rows
+    wide = current.shape[1] - rows
     writes_out[...] = current[:, :wide]
-    for out, part in ((inverse_out, current[:, wide : wide + rows]), (scaled_out, current[:, wide + rows :])):
-        out[...] = part.astype(BF16)
+    inverse = current[:, wide:]
+    inverse_out[...] = inverse.astype(BF16)
+    scaled_out[...] = (inverse * jnp.sum(jnp.where(same, weights, 0.0), axis=0, keepdims=True)).astype(BF16)
 
 
 def next_kernel(starts_ref, keys_ref, writes_ref, matrix_ref, totals_ref, matrix_out, totals_out):
@@ -244,18 +241,19 @@
     return [pltpu.make_async_copy(matrix_ref.at[pl.ds(z * wide, wide)], held_ref.at[z], arrived.at[z, 0])]
 
 
-def away_copies(z, place_ref, held_ref, arrived, matrix_ref, bulk_ref):
-    few = bulk_ref.shape[1]
+def away_copies(z, place_ref, held_ref, arrived, matrix_ref, mine_ref, theirs_ref):
+    few = mine_ref.shape[1]
     width = held_ref.shape[1] // 2
     many = width - few
+    core = place_ref[0] % 2
     return [
         pltpu.make_async_copy(source, held_ref.at[z, pl.ds(start, size)], arrived.at[z, number])
         for number, (source, start, size) in enumerate(
             (
                 (matrix_ref.at[pl.ds(2 * z * many, many)], 0, many),
-                (bulk_ref.at[2 * z], many, few),
                 (matrix_ref.at[pl.ds((2 * z + 1) * many, many)], width, many),
-                (bulk_ref.at[2 * z + 1], width + many, few),
+                (mine_ref.at[z], pl.multiple_of(core * width + many, few), few),
+                (theirs_ref.at[z], pl.multiple_of((1 - core) * width + many, few), few),
             )
         )
     ]
@@ -276,7 +274,7 @@
     width = mine_ref.shape[2]
     base = dot(probe_ref[...], held_ref[step], ((1,), (1,)))
     scale = scale_ref[:, :1]
-    swap = place_ref[1] == 1
+    swap = place_ref[0] % 2 == 1
     for side in range(2):
         cols = slice(side * width, (side + 1) * width)
         writes = jnp.where(swap == (side == 0), theirs_ref[0], mine_ref[0])
@@ -287,17 +285,22 @@
 def read_half(half, me, probe, mix, scale, entering, values, matrices, copies, previous=None):
     count, depth = probe.shape
     rows, width = values[0].shape[1:]
-    distance = (jnp.arange(4, dtype=jnp.int32) - me // 4) % 4
-    slot_of = jnp.where(distance == 3, 1, jnp.where(distance == 0, 0, distance + 1))
-    place = jnp.concatenate([jnp.stack([half, me % 2]), slot_of])
-    args = [place, probe, mix, scale, entering, *values, *matrices]
+
+    def half_of(place):
+        return (place[0] // 2 + half) % 2
+
+    def slot_of(z, place):
+        distance = (z + 4 - place[0] // 4) % 4
+        return jnp.where(distance == 3, 1, jnp.where(distance == 0, 0, distance + 1))
+
+    args = [me, probe, mix, scale, entering, *values, *matrices]
     specs = [
         pl.BlockSpec((count, depth), lambda z, p: (0, 0)),
         pl.BlockSpec((count, rows), lambda z, p: (0, 0)),
         pl.BlockSpec((count, 128), lambda z, p: (0, 0)),
-        pl.BlockSpec((count, 2 * width), lambda z, p: (0, 2 * z + p[0])),
-        pl.BlockSpec((1, rows, width), lambda z, p: (p[2 + z], 0, 0)),
-        pl.BlockSpec((1, rows, width), lambda z, p: (p[2 + z], 0, 0)),
+        pl.BlockSpec((count, 2 * width), lambda z, p: (0, 2 * z + half_of(p))),
+        pl.BlockSpec((1, rows, width), lambda z, p: (slot_of(z, p), 0, 0)),
+        pl.BlockSpec((1, rows, width), lambda z, p: (slot_of(z, p), 0, 0)),
     ] + [pl.BlockSpec(memory_space=pl.ANY)] * len(matrices)
     if previous is not None:
         args.append(previous)
@@ -309,7 +312,7 @@
             num_scalar_prefetch=1,
             grid=(4,),
             in_specs=specs,
-            out_specs=pl.BlockSpec((count, 2 * width), lambda z, p: (0, 2 * z + p[0])),
+            out_specs=pl.BlockSpec((count, 2 * width), lambda z, p: (0, 2 * z + half_of(p))),
             scratch_shapes=[pltpu.VMEM((4, 2 * width, depth), BF16), pltpu.SemaphoreType.DMA((4, 4))],
         ),
         input_output_aliases={} if previous is None else {len(args) - 1: 0},
@@ -330,8 +333,6 @@
 
 def local(leaving, w_query, w_key, w_value, w_gate, norm_gain, memory_matrix, key_totals, doc_starts):
     me = lax.axis_index("seg").astype(jnp.int32)
-    slots = slot_segments(me, offsets())
-    pair_slots = slot_segments(me, pair_offsets())
     mine = jnp.full((1,), me)
     leaving, matrix = leaving[0, 0], memory_matrix[0]
     width, features, depth = matrix.shape[0], leaving.shape[1], matrix.shape[1]
@@ -341,11 +342,14 @@
     entering = shifted_rows(leaving)
     groups = [[i for i in range(16) if (i // 2) % 2 == y] for y in (0, 1)]
     near = lax.all_gather(matrix, "seg", axis=0, tiled=True, axis_index_groups=groups)
-    trimmed = matrix[: 7 * width // 8]
+    trimmed = matrix[: 3 * width // 4]
     partner = permute(trimmed, "seg", lambda i: i ^ 2)
     away = lax.all_gather(partner, "seg", axis=0, tiled=True, axis_index_groups=groups)
-    bulk = near.reshape(8, width, depth)[:, 7 * width // 8 :]
+    bulk = lax.dynamic_slice(
+        near.reshape(4, 2, width, depth), (0, me % 2, 3 * width // 4, 0), (4, 1, width // 4, depth)
+    )[:, 0]
     bulk = permute(bulk, "seg", lambda i: i ^ 2)
+    twin = permute(bulk, "seg", lambda i: i ^ 1)
 
     normed = call(
         norm_kernel, shape((2, MEM, features), BF16), head, across, norm_gain, specs=[VM] * 3
@@ -359,7 +363,7 @@
             shape((rows, width), BF16),
             shape((rows, 128), F32),
         ),
-        pair_slots, *memory, w_key[0], w_value[0], w_gate,
+        mine, *memory, w_key[0], w_value[0], w_gate,
         specs=[SM] + [VM] * 11,
     )
     pieces = gather_slots(key_part)
@@ -367,7 +371,7 @@
     keys, writes, inverse, scaled = call(
         solve_kernel,
         (shape((rows, depth), BF16), shape((rows, width), F32), shape((rows, rows), BF16), shape((rows, rows), BF16)),
-        slots, doc_starts, *pieces, values, rates, matrix, key_totals,
+        mine, doc_starts, *pieces, values, rates, matrix, key_totals,
         specs=[SM, SM] + [VM] * 8,
     )
     matrix_next, totals_next = call(
@@ -378,7 +382,7 @@
     )
 
     count = leaving.shape[0]
-    any_space = pl.BlockSpec(memory_space=pl.ANY)
+    any_space = pl.BlockSpec(memory_space=pl.ANY if INTERPRET else pltpu.HBM)
     block = depth // 4
     queries, entering = pl.pallas_call(
         query_kernel,
@@ -404,10 +408,9 @@
         mine, doc_starts, queries, keys, key_totals, inverse, scaled,
         specs=[SM, SM] + [VM] * 5,
     )
-    half = (me // 2) % 2
-    parts = (me, probe, mix, scale, entering)
-    updated = read_half(half, *parts, value_slots[0::2], (near,), near_copies)
-    updated = read_half(1 - half, *parts, value_slots[1::2], (away, bulk), away_copies, updated)
+    parts = (mine, probe, mix, scale, entering)
+    updated = read_half(0, *parts, value_slots[0::2], (near,), near_copies)
+    updated = read_half(1, *parts, value_slots[1::2], (away, bulk, twin), away_copies, updated)
     return updated[None, None], matrix_next[None], totals_next
 
 

time: 235 us -> 217 us (0.923)
  waiting for transfers between devices: 119 us -> 107 us
  other arithmetic: 4.71 us -> 0.94 us
    ppermute x22 -> x23, waiting for transfers between devices: 115 us -> 103 us  [permute(): return lax.ppermute(block, axis, [(i, target(i)) for i in range(size)])]
    ppermute x22 -> x23, starting transfers between devices: 26.7 us -> 30 us  [permute(): return lax.ppermute(block, axis, [(i, target(i)) for i in range(size)])]
    slice x2 -> x1, local copies, waits for them, and re-layouts: 3.66 us -> 1.2 us  [local(): trimmed = matrix[:3 * width // 4]]
  transfers between devices with their start and end apart: 29 -> 30, of which waited for: 13 -> 15; matrix products, arithmetic and copies ran while one was open for 4% -> 2% of each run, Pallas kernels for 18% -> 19%
where the time goes in v2:
time: 217 us; the launch traced here: 216 us
  waiting for transfers between devices  107 us (49%)
  Pallas kernels  50 us (23%)
  starting transfers between devices  39 us (18%)
  between operations  14.3 us (7%)
  local copies, waits for them, and re-layouts  5 us (2%)
    ppermute x23, waiting for transfers between devices, permute(): return lax.ppermute(block, axis, [(i, target(i)) for i in range(size)])  103 us
    ppermute x23, starting transfers between devices, permute(): return lax.ppermute(block, axis, [(i, target(i)) for i in range(size)])  30 us
    pallas_call x5, Pallas kernels, call(): pl.pallas_call(kernel, out_shape=outs, in_specs=list(specs), out_specs=ja...  20.4 us
    pallas_call x2, Pallas kernels, read_half(): pl.pallas_call(functools.partial(read_kernel, copies, len(matrices)), out...  16.2 us
    pallas_call x1, Pallas kernels, local(): pl.pallas_call(query_kernel, out_shape=(shape((count, depth), BF16), shap...  13.5 us
    ppermute x4, starting transfers between devices, send(): lax.ppermute(part, ('seg', 'section'), [(s * wide + p, s * wide + q) for...  6.76 us
  transfers between devices with their start and end apart: 30, of which 15 were waited for; matrix products, arithmetic and copies ran while one was open for 2% of the time, Pallas kernels for 19%

profile of v2, /device:TPU:1, one launch (start us, length us, event | category | flops | bytes accessed | tf_op | source)
XLA Modules:
  0.0 216.3 jit_solution(12414828023772487667)
XLA Ops:
  7.2 0.7 all-gather.6.cloned.1.call-update
  7.9 1.2 slice_bitcast_fusion
  9.2 2.2 %collective-permute-start.24 = (bf16[192,2048]{1,0:T(8,128)(2,1)S(1)}, bf16[192,2048]{1,0:T(8,128)(2,1)S(1)}, u32[]{:S(2)}, u32[]{:S(2)}) collective-permute-start(bf16[192,2048]{1,0:T(8,128)(2,1)S(1)} %slice_bitcast_fusion), channel_id=1, source_target_pairs={{0,16},{8,24},{16,0},{24,8},{32,48},{40,56},{48,32},{56,40},{64,80... | collective-permute-start | bytes 2359304 | tf_op jit(solution)/shard_map/ppermute | solution.py:24
  11.3 17.0 %collective-permute-done.24 = bf16[192,2048]{1,0:T(8,128)(2,1)S(1)} collective-permute-done((bf16[192,2048]{1,0:T(8,128)(2,1)S(1)}, bf16[192,2048]{1,0:T(8,128)(2,1)S(1)}, u32[]{:S(2)}, u32[]{:S(2)}) %collective-permute-start.24) | collective-permute-done | bytes 786464 | tf_op jit(solution)/shard_map/ppermute | solution.py:24
  28.4 0.9 copy-done.3
  29.3 2.0 collective-permute-start.2
  31.3 0.9 slice_bitcast_fusion.1
  32.2 1.5 collective-permute-start.4
  33.7 2.2 %collective-permute-start.5 = (bf16[16,4096]{1,0:T(8,128)(2,1)S(1)}, bf16[16,4096]{1,0:T(8,128)(2,1)S(1)}, u32[]{:S(2)}, u32[]{:S(2)}) collective-permute-start(bf16[16,4096]{1,0:T(8,128)(2,1)S(1)} %slice_bitcast_fusion.1), channel_id=1, source_target_pairs={{0,17},{1,18},{2,19},{3,20},{4,21},{5,22},{6,23},{7,16},{8,25},{9,... | collective-permute-start | bytes 393224 | tf_op jit(solution)/shard_map/ppermute | solution.py:38
  35.9 4.0 %collective-permute-done.4.rows_ref = bf16[16,4096]{1,0:T(8,128)(2,1)S(1)} collective-permute-done((bf16[16,4096]{1,0:T(8,128)(2,1)S(1)}, bf16[16,4096]{1,0:T(8,128)(2,1)S(1)}, u32[]{:S(2)}, u32[]{:S(2)}) %collective-permute-start.4) | collective-permute-done | bytes 131104 | tf_op jit(solution)/shard_map/ppermute | solution.py:24
  39.9 3.3 %collective-permute-done.5.across_ref = bf16[16,4096]{1,0:T(8,128)(2,1)S(1)} collective-permute-done((bf16[16,4096]{1,0:T(8,128)(2,1)S(1)}, bf16[16,4096]{1,0:T(8,128)(2,1)S(1)}, u32[]{:S(2)}, u32[]{:S(2)}) %collective-permute-start.5) | collective-permute-done | bytes 131104 | tf_op jit(solution)/shard_map/ppermute | solution.py:38
  43.9 1.8 shard_map.113.refs_0_
  45.7 1.8 collective-permute-start.6
  47.5 2.1 collective-permute-start.7
  49.7 1.3 collective-permute-start.8
  50.9 3.0 %collective-permute-start.9 = (bf16[2,16,4096]{2,1,0:T(8,128)(2,1)}, bf16[2,16,4096]{2,1,0:T(8,128)(2,1)S(1)}, u32[]{:S(2)}, u32[]{:S(2)}) collective-permute-start(bf16[2,16,4096]{2,1,0:T(8,128)(2,1)} %shard_map.113.refs_0_), channel_id=1, source_target_pairs={{0,8},{8,0},{16,24},{24,16},{32,40},{40,32},{48,56},{56,48},{64,72... | collective-permute-start | bytes 786440 | tf_op jit(solution)/shard_map/ppermute | solution.py:24
  54.0 7.9 %collective-permute-done.6.refs_1_ = bf16[2,16,4096]{2,1,0:T(8,128)(2,1)S(1)} collective-permute-done((bf16[2,16,4096]{2,1,0:T(8,128)(2,1)}, bf16[2,16,4096]{2,1,0:T(8,128)(2,1)S(1)}, u32[]{:S(2)}, u32[]{:S(2)}) %collective-permute-start.6) | collective-permute-done | bytes 262176 | tf_op jit(solution)/shard_map/ppermute | solution.py:24
  61.8 1.4 collective-permute-start
  63.3 2.9 %collective-permute-start.10 = (bf16[2,16,4096]{2,1,0:T(8,128)(2,1)S(1)}, bf16[2,16,4096]{2,1,0:T(8,128)(2,1)S(1)}, u32[]{:S(2)}, u32[]{:S(2)}) collective-permute-start(bf16[2,16,4096]{2,1,0:T(8,128)(2,1)S(1)} %collective-permute-done.6.refs_1_), channel_id=1, source_target_pairs={{0,8},{8,0},{16,24},{24,16},{32,40},{40,32},{48,56},{56,48},{64,72... | collective-permute-start | bytes 786440 | tf_op jit(solution)/shard_map/ppermute | solution.py:24
  66.2 5.6 %collective-permute-done.8.refs_3_ = bf16[2,16,4096]{2,1,0:T(8,128)(2,1)S(1)} collective-permute-done((bf16[2,16,4096]{2,1,0:T(8,128)(2,1)}, bf16[2,16,4096]{2,1,0:T(8,128)(2,1)S(1)}, u32[]{:S(2)}, u32[]{:S(2)}) %collective-permute-start.8) | collective-permute-done | bytes 262176 | tf_op jit(solution)/shard_map/ppermute | solution.py:24
  71.9 1.2 collective-permute-start.11
  73.2 1.2 collective-permute-done.11.refs_6_
  74.8 5.2 %shard_map.114 = (bf16[256,128]{1,0:T(8,128)(2,1)}, f32[256,256]{1,0:T(8,128)}, bf16[256,256]{1,0:T(8,128)(2,1)}, f32[256,128]{1,0:T(8,128)}) custom-call(s32[1]{0:T(128)} %bitcast.me_ref.place_ref, bf16[2,16,4096]{2,1,0:T(8,128)(2,1)} %shard_map.113.refs_0_, bf16[2,16,4096]{2,1,0:T(8,128)(2,1)} %copy-done.8, bf16[2,16,4096]{2,1,0:T(8,128)(2,1)} %copy-done.9, ...), custom_call_target="tpu_custom_call" | custom-call | tf_op jit(solution)/shard_map/pallas_call | solution.py:324
  80.1 1.9 collective-permute-start.13
  82.0 1.4 collective-permute-start.14
  83.4 1.5 collective-permute-done.15
  84.8 2.0 collective-permute-start.1
  87.1 0.8 collective-permute-start.19
  87.9 1.9 collective-permute-start.20
  89.7 1.3 collective-permute-start.3
  91.1 1.3 dynamic-slice_bitcast_fusion
  92.4 4.1 %collective-permute-done.19 = bf16[256,256]{1,0:T(8,128)(2,1)S(1)} collective-permute-done((bf16[256,256]{1,0:T(8,128)(2,1)}, bf16[256,256]{1,0:T(8,128)(2,1)S(1)}, u32[]{:S(2)}, u32[]{:S(2)}) %collective-permute-start.19) | collective-permute-done | bytes 131104 | tf_op jit(solution)/shard_map/ppermute | solution.py:24
  96.4 1.0 collective-permute-start.25
  97.4 0.9 pad_maximum_fusion.1.a_ref
  98.3 8.5 %collective-permute-done.21 = bf16[256,256]{1,0:T(8,128)(2,1)S(1)} collective-permute-done((bf16[256,256]{1,0:T(8,128)(2,1)}, bf16[256,256]{1,0:T(8,128)(2,1)S(1)}, u32[]{:S(2)}, u32[]{:S(2)}) %collective-permute-start.21) | collective-permute-done | bytes 131104 | tf_op jit(solution)/shard_map/ppermute | solution.py:24
  107.4 39.1 %collective-permute-done.16.b_ref = bf16[4,256,128]{2,1,0:T(8,128)(2,1)S(1)} collective-permute-done((bf16[4,256,128]{2,1,0:T(8,128)(2,1)S(1)}, bf16[4,256,128]{2,1,0:T(8,128)(2,1)S(1)}, u32[]{:S(2)}, u32[]{:S(2)}) %collective-permute-start.16) | collective-permute-done | bytes 262176 | tf_op jit(solution)/shard_map/ppermute | solution.py:24
  146.5 1.7 collective-permute-start.17
  148.2 1.2 collective-permute-done.17.c_ref
  149.8 1.1 collective-permute-done.18.d_ref
  150.9 2.2 %collective-permute-start.22 = (bf16[4,256,256]{2,1,0:T(8,128)(2,1)S(1)}, bf16[4,256,256]{2,1,0:T(8,128)(2,1)S(1)}, u32[]{:S(2)}, u32[]{:S(2)}) collective-permute-start(bf16[4,256,256]{2,1,0:T(8,128)(2,1)S(1)} %pad_maximum_fusion.mine_ref), channel_id=1, source_target_pairs={{0,16},{8,24},{16,0},{24,8},{32,48},{40,56},{48,32},{56,40},{64,80... | collective-permute-start | bytes 1572872 | tf_op jit(solution)/shard_map/ppermute | solution.py:24
  153.7 11.3 %collective-permute-done.22.mine_ref = bf16[4,256,256]{2,1,0:T(8,128)(2,1)S(1)} collective-permute-done((bf16[4,256,256]{2,1,0:T(8,128)(2,1)S(1)}, bf16[4,256,256]{2,1,0:T(8,128)(2,1)S(1)}, u32[]{:S(2)}, u32[]{:S(2)}) %collective-permute-start.22) | collective-permute-done | bytes 524320 | tf_op jit(solution)/shard_map/ppermute | solution.py:24
  165.0 0.9 collective-permute-start.27
  166.3 6.0 %shard_map.115 = (bf16[256,2048]{1,0:T(8,128)(2,1)}, f32[256,256]{1,0:T(8,128)}, bf16[256,256]{1,0:T(8,128)(2,1)}, bf16[256,256]{1,0:T(8,128)(2,1)}) custom-call(s32[1]{0:T(128)} %bitcast.me_ref.place_ref, s32[1,16]{1,0:T(1,128)} %starts_ref.5, bf16[4,256,128]{2,1,0:T(8,128)(2,1)} %copy-done.2, bf16[4,256,128]{2,1,0:T(8,128)(2,1)} %copy-done.5, ...), custom_call_target="tpu_custom_call" | custom-call | tf_op jit(solution)/shard_map/pallas_call | solution.py:324
  172.4 3.1 %shard_map.119 = (bf16[256,2048]{1,0:T(8,128)(2,1)}, f32[1,2048]{1,0:T(1,128)}) custom-call(s32[1,16]{1,0:T(1,128)} %starts_ref.5, bf16[256,2048]{1,0:T(8,128)(2,1)} %get-tuple-element.22.keys_ref, f32[256,256]{1,0:T(8,128)} %get-tuple-element.30.writes_ref, bf16[256,2048]{1,0:T(8,128)(2,1)} %bitcast.29, f32[1,2048]{1,0:T(1,128)} %totals_ref.5), custom_call_target="tpu_custom_call" | custom-call | tf_op jit(solution)/shard_map/pallas_call | solution.py:324
  175.5 13.5 %shard_map.112 = (bf16[272,2048]{1,0:T(8,128)(2,1)}, bf16[272,4096]{1,0:T(8,128)(2,1)}) custom-call(s32[1]{0:T(128)} %bitcast.1.source_ref, bf16[272,4096]{1,0:T(8,128)(2,1)} %copy-done, bf16[272,4096]{1,0:T(8,128)(2,1)} %collective-permute-done.1.second_ref, bf16[272,4096]{1,0:T(8,128)(2,1)} %collective-permute-done.3.third_ref, bf16[1,4096]{1,0:T(2,128)(2,1)} %gain_ref.3, ...), custom_call_target="tpu_custom_call" | custom-call | tf_op jit(solution)/shard_map/pallas_call | solution.py:387
  189.0 4.2 %shard_map.116 = (bf16[272,2048]{1,0:T(8,128)(2,1)}, bf16[272,256]{1,0:T(8,128)(2,1)}, f32[272,128]{1,0:T(8,128)}) custom-call(s32[1]{0:T(128)} %bitcast.me_ref.place_ref, s32[1,16]{1,0:T(1,128)} %starts_ref.5, bf16[272,2048]{1,0:T(8,128)(2,1)} %get-tuple-element.18.queries_ref, bf16[256,2048]{1,0:T(8,128)(2,1)} %get-tuple-element.22.keys_ref, ...), custom_call_target="tpu_custom_call" | custom-call | tf_op jit(solution)/shard_map/pallas_call | solution.py:324
  193.2 8.1 %shard_map.117.rest_3_ = bf16[272,4096]{1,0:T(8,128)(2,1)} custom-call(s32[1]{0:T(128)} %bitcast.me_ref.place_ref, bf16[272,2048]{1,0:T(8,128)(2,1)} %get-tuple-element.25.probe_ref, bf16[272,256]{1,0:T(8,128)(2,1)} %get-tuple-element.26.mix_ref, f32[272,128]{1,0:T(8,128)} %get-tuple-element.27.scale_ref, bf16[272,4096]{1,0:T(8,128)(2,1)} %get-tuple-element.28.rows_ref, ...), custom_call_target="tpu_custom_call" | custom-call | tf_op jit(solution)/shard_map/pallas_call | solution.py:308
  201.3 8.1 %shard_map.118 = bf16[272,4096]{1,0:T(8,128)(2,1)} custom-call(s32[1]{0:T(128)} %bitcast.me_ref.place_ref, bf16[272,2048]{1,0:T(8,128)(2,1)} %get-tuple-element.25.probe_ref, bf16[272,256]{1,0:T(8,128)(2,1)} %get-tuple-element.26.mix_ref, f32[272,128]{1,0:T(8,128)} %get-tuple-element.27.scale_ref, ...), custom_call_target="tpu_custom_call", output_to_operand_aliasing={{}: (10, {})} | custom-call | tf_op jit(solution)/shard_map/pallas_call | solution.py:308
  (59 shorter events, 3.7 us)
Async XLA Ops:
  7.2 83.9 %all-gather.6.cloned.1.call-start = ((), (), s32[]{:S(2)}) async-start(), calls=%async_computation.1 | async-start | bytes 9437184 | tf_op jit(solution)/shard_map/all_gather | solution.py:344
  7.9 193.4 %all-gather.4.cloned.1.call-start = ((), (), s32[]{:S(2)}) async-start(), calls=%async_computation | async-start | bytes 7077888 | tf_op jit(solution)/shard_map/all_gather | solution.py:347
  9.2 19.2 %collective-permute-start.24 = (bf16[192,2048]{1,0:T(8,128)(2,1)S(1)}, bf16[192,2048]{1,0:T(8,128)(2,1)S(1)}, u32[]{:S(2)}, u32[]{:S(2)}) collective-permute-start(bf16[192,2048]{1,0:T(8,128)(2,1)S(1)} %slice_bitcast_fusion), channel_id=1, source_target_pairs={{0,16},{8,24},{16,0},{24,8},{32,48},{40,56},{48,32},{56,40},{64,80... | collective-permute-start | bytes 2359304 | tf_op jit(solution)/shard_map/ppermute | solution.py:24
  28.4 0.9 copy-start.3
  29.3 60.5 %collective-permute-start.2 = (bf16[272,4096]{1,0:T(8,128)(2,1)}, bf16[272,4096]{1,0:T(8,128)(2,1)}, u32[]{:S(2)}, u32[]{:S(2)}) collective-permute-start(bf16[272,4096]{1,0:T(8,128)(2,1)} %bitcast.43), channel_id=1, source_target_pairs={{11,15},{15,11},{19,23},{23,19},{43,47},{47,43},{51,55},{55,51},{7... | collective-permute-start | bytes 6684680 | tf_op jit(solution)/shard_map/ppermute | solution.py:48
  32.2 7.7 %collective-permute-start.4 = (bf16[16,4096]{1,0:T(8,128)(2,1)S(1)}, bf16[16,4096]{1,0:T(8,128)(2,1)S(1)}, u32[]{:S(2)}, u32[]{:S(2)}) collective-permute-start(bf16[16,4096]{1,0:T(8,128)(2,1)S(1)} %slice_bitcast_fusion.1), channel_id=1, source_target_pairs={{0,1},{1,2},{2,3},{3,4},{4,5},{5,6},{6,7},{7,0},{8,9},{9,10},{10,1... | collective-permute-start | bytes 393224 | tf_op jit(solution)/shard_map/ppermute | solution.py:24
  33.7 9.5 %collective-permute-start.5 = (bf16[16,4096]{1,0:T(8,128)(2,1)S(1)}, bf16[16,4096]{1,0:T(8,128)(2,1)S(1)}, u32[]{:S(2)}, u32[]{:S(2)}) collective-permute-start(bf16[16,4096]{1,0:T(8,128)(2,1)S(1)} %slice_bitcast_fusion.1), channel_id=1, source_target_pairs={{0,17},{1,18},{2,19},{3,20},{4,21},{5,22},{6,23},{7,16},{8,25},{9,... | collective-permute-start | bytes 393224 | tf_op jit(solution)/shard_map/ppermute | solution.py:38
  39.9 3.3 %copy-start.13 = (bf16[16,4096]{1,0:T(8,128)(2,1)}, bf16[16,4096]{1,0:T(8,128)(2,1)S(1)}, u32[]{:S(2)}) copy-start(bf16[16,4096]{1,0:T(8,128)(2,1)S(1)} %collective-permute-done.4.rows_ref) | copy-start | bytes 393220
  43.2 0.7 copy-start.14
  45.7 16.1 %collective-permute-start.6 = (bf16[2,16,4096]{2,1,0:T(8,128)(2,1)}, bf16[2,16,4096]{2,1,0:T(8,128)(2,1)S(1)}, u32[]{:S(2)}, u32[]{:S(2)}) collective-permute-start(bf16[2,16,4096]{2,1,0:T(8,128)(2,1)} %shard_map.113.refs_0_), channel_id=1, source_target_pairs={{0,32},{8,40},{16,48},{24,56},{32,64},{40,72},{48,80},{56,88},{64,... | collective-permute-start | bytes 786440 | tf_op jit(solution)/shard_map/ppermute | solution.py:24
  47.5 15.8 %collective-permute-start.7 = (bf16[2,16,4096]{2,1,0:T(8,128)(2,1)}, bf16[2,16,4096]{2,1,0:T(8,128)(2,1)S(1)}, u32[]{:S(2)}, u32[]{:S(2)}) collective-permute-start(bf16[2,16,4096]{2,1,0:T(8,128)(2,1)} %shard_map.113.refs_0_), channel_id=1, source_target_pairs={{0,96},{8,104},{16,112},{24,120},{32,0},{40,8},{48,16},{56,24},{64... | collective-permute-start | bytes 786440 | tf_op jit(solution)/shard_map/ppermute | solution.py:24
  49.7 22.2 %collective-permute-start.8 = (bf16[2,16,4096]{2,1,0:T(8,128)(2,1)}, bf16[2,16,4096]{2,1,0:T(8,128)(2,1)S(1)}, u32[]{:S(2)}, u32[]{:S(2)}) collective-permute-start(bf16[2,16,4096]{2,1,0:T(8,128)(2,1)} %shard_map.113.refs_0_), channel_id=1, source_target_pairs={{0,64},{8,72},{16,80},{24,88},{32,96},{40,104},{48,112},{56,120},{... | collective-permute-start | bytes 786440 | tf_op jit(solution)/shard_map/ppermute | solution.py:24
  50.9 22.2 %collective-permute-start.9 = (bf16[2,16,4096]{2,1,0:T(8,128)(2,1)}, bf16[2,16,4096]{2,1,0:T(8,128)(2,1)S(1)}, u32[]{:S(2)}, u32[]{:S(2)}) collective-permute-start(bf16[2,16,4096]{2,1,0:T(8,128)(2,1)} %shard_map.113.refs_0_), channel_id=1, source_target_pairs={{0,8},{8,0},{16,24},{24,16},{32,40},{40,32},{48,56},{56,48},{64,72... | collective-permute-start | bytes 786440 | tf_op jit(solution)/shard_map/ppermute | solution.py:24
  61.8 12.9 %copy-start.8 = (bf16[2,16,4096]{2,1,0:T(8,128)(2,1)}, bf16[2,16,4096]{2,1,0:T(8,128)(2,1)S(1)}, u32[]{:S(2)}) copy-start(bf16[2,16,4096]{2,1,0:T(8,128)(2,1)S(1)} %collective-permute-done.6.refs_1_) | copy-start | bytes 786436
  61.8 104.1 %collective-permute-start = (bf16[272,4096]{1,0:T(8,128)(2,1)}, bf16[272,4096]{1,0:T(8,128)(2,1)S(1)}, u32[]{:S(2)}, u32[]{:S(2)}) collective-permute-start(bf16[272,4096]{1,0:T(8,128)(2,1)} %bitcast.44), channel_id=1, source_target_pairs={{0,1},{1,2},{2,3},{4,5},{5,6},{6,7},{8,9},{9,10},{10,11},{12,13},{... | collective-permute-start | bytes 6684680 | tf_op jit(solution)/shard_map/ppermute | solution.py:48
  63.3 11.5 %copy-start.9 = (bf16[2,16,4096]{2,1,0:T(8,128)(2,1)}, bf16[2,16,4096]{2,1,0:T(8,128)(2,1)S(1)}, u32[]{:S(2)}) copy-start(bf16[2,16,4096]{2,1,0:T(8,128)(2,1)S(1)} %collective-permute-done.7.refs_2_) | copy-start | bytes 786436
  63.3 9.9 %collective-permute-start.10 = (bf16[2,16,4096]{2,1,0:T(8,128)(2,1)S(1)}, bf16[2,16,4096]{2,1,0:T(8,128)(2,1)S(1)}, u32[]{:S(2)}, u32[]{:S(2)}) collective-permute-start(bf16[2,16,4096]{2,1,0:T(8,128)(2,1)S(1)} %collective-permute-done.6.refs_1_), channel_id=1, source_target_pairs={{0,8},{8,0},{16,24},{24,16},{32,40},{40,32},{48,56},{56,48},{64,72... | collective-permute-start | bytes 786440 | tf_op jit(solution)/shard_map/ppermute | solution.py:24
  71.9 2.9 %copy-start.10 = (bf16[2,16,4096]{2,1,0:T(8,128)(2,1)}, bf16[2,16,4096]{2,1,0:T(8,128)(2,1)S(1)}, u32[]{:S(2)}) copy-start(bf16[2,16,4096]{2,1,0:T(8,128)(2,1)S(1)} %collective-permute-done.8.refs_3_) | copy-start | bytes 786436
  71.9 2.5 %collective-permute-start.11 = (bf16[2,16,4096]{2,1,0:T(8,128)(2,1)S(1)}, bf16[2,16,4096]{2,1,0:T(8,128)(2,1)}, u32[]{:S(2)}, u32[]{:S(2)}) collective-permute-start(bf16[2,16,4096]{2,1,0:T(8,128)(2,1)S(1)} %collective-permute-done.7.refs_2_), channel_id=1, source_target_pairs={{0,8},{8,0},{16,24},{24,16},{32,40},{40,32},{48,56},{56,48},{64,72... | collective-permute-start | bytes 786440 | tf_op jit(solution)/shard_map/ppermute | solution.py:24
  73.1 1.7 copy-start.11
  73.1 1.7 collective-permute-start.12
  73.2 1.6 copy-start.12
  80.0 69.8 %copy-start.15 = (bf16[256,256]{1,0:T(8,128)(2,1)S(1)}, bf16[256,256]{1,0:T(8,128)(2,1)}, u32[]{:S(2)}) copy-start(bf16[256,256]{1,0:T(8,128)(2,1)} %get-tuple-element.29) | copy-start | bytes 393220
  80.0 4.9 %collective-permute-start.15 = (bf16[256,128]{1,0:T(8,128)(2,1)}, bf16[256,128]{1,0:T(8,128)(2,1)S(1)}, u32[]{:S(2)}, u32[]{:S(2)}) collective-permute-start(bf16[256,128]{1,0:T(8,128)(2,1)} %get-tuple-element.19), channel_id=1, source_target_pairs={{0,64},{8,72},{16,80},{24,88},{32,96},{40,104},{48,112},{56,120},{... | collective-permute-start | bytes 196616 | tf_op jit(solution)/shard_map/ppermute | solution.py:24
  80.1 7.0 %collective-permute-start.13 = (bf16[256,128]{1,0:T(8,128)(2,1)}, bf16[256,128]{1,0:T(8,128)(2,1)S(1)}, u32[]{:S(2)}, u32[]{:S(2)}) collective-permute-start(bf16[256,128]{1,0:T(8,128)(2,1)} %get-tuple-element.19), channel_id=1, source_target_pairs={{0,32},{8,40},{16,48},{24,56},{32,64},{40,72},{48,80},{56,88},{64,... | collective-permute-start | bytes 196616 | tf_op jit(solution)/shard_map/ppermute | solution.py:24
  82.0 5.9 %collective-permute-start.14 = (bf16[256,128]{1,0:T(8,128)(2,1)}, bf16[256,128]{1,0:T(8,128)(2,1)S(1)}, u32[]{:S(2)}, u32[]{:S(2)}) collective-permute-start(bf16[256,128]{1,0:T(8,128)(2,1)} %get-tuple-element.19), channel_id=1, source_target_pairs={{0,96},{8,104},{16,112},{24,120},{32,0},{40,8},{48,16},{56,24},{64... | collective-permute-start | bytes 196616 | tf_op jit(solution)/shard_map/ppermute | solution.py:24
  84.8 90.7 %collective-permute-start.1 = (bf16[272,4096]{1,0:T(8,128)(2,1)}, bf16[272,4096]{1,0:T(8,128)(2,1)}, u32[]{:S(2)}, u32[]{:S(2)}) collective-permute-start(bf16[272,4096]{1,0:T(8,128)(2,1)} %bitcast.45), channel_id=1, source_target_pairs={{3,4},{7,0},{27,28},{31,24},{35,36},{39,32},{59,60},{63,56},{67,68... | collective-permute-start | bytes 6684680 | tf_op jit(solution)/shard_map/ppermute | solution.py:48
  87.1 9.4 %collective-permute-start.19 = (bf16[256,256]{1,0:T(8,128)(2,1)}, bf16[256,256]{1,0:T(8,128)(2,1)S(1)}, u32[]{:S(2)}, u32[]{:S(2)}) collective-permute-start(bf16[256,256]{1,0:T(8,128)(2,1)} %get-tuple-element.29), channel_id=1, source_target_pairs={{0,32},{8,40},{16,48},{24,56},{32,64},{40,72},{48,80},{56,88},{64,... | collective-permute-start | bytes 393224 | tf_op jit(solution)/shard_map/ppermute | solution.py:24
  87.9 9.6 %collective-permute-start.20 = (bf16[256,256]{1,0:T(8,128)(2,1)}, bf16[256,256]{1,0:T(8,128)(2,1)S(1)}, u32[]{:S(2)}, u32[]{:S(2)}) collective-permute-start(bf16[256,256]{1,0:T(8,128)(2,1)} %get-tuple-element.29), channel_id=1, source_target_pairs={{0,96},{8,104},{16,112},{24,120},{32,0},{40,8},{48,16},{56,24},{64... | collective-permute-start | bytes 393224 | tf_op jit(solution)/shard_map/ppermute | solution.py:24
  89.7 85.7 %collective-permute-start.3 = (bf16[272,4096]{1,0:T(8,128)(2,1)}, bf16[272,4096]{1,0:T(8,128)(2,1)}, u32[]{:S(2)}, u32[]{:S(2)}) collective-permute-start(bf16[272,4096]{1,0:T(8,128)(2,1)} %collective-permute-done.2), channel_id=1, source_target_pairs={{11,8},{15,12},{19,16},{23,20},{43,40},{47,44},{51,48},{55,52},{75... | collective-permute-start | bytes 6684680 | tf_op jit(solution)/shard_map/ppermute | solution.py:48
  96.4 56.6 %collective-permute-start.25 = (bf16[4,64,2048]{2,1,0:T(8,128)(2,1)S(1)}, bf16[4,64,2048]{2,1,0:T(8,128)(2,1)}, u32[]{:S(2)}, u32[]{:S(2)}) collective-permute-start(bf16[4,64,2048]{2,1,0:T(8,128)(2,1)S(1)} %dynamic-slice_bitcast_fusion), channel_id=1, source_target_pairs={{0,16},{8,24},{16,0},{24,8},{32,48},{40,56},{48,32},{56,40},{64,80... | collective-permute-start | bytes 3145736 | tf_op jit(solution)/shard_map/ppermute | solution.py:24
  97.4 9.4 %collective-permute-start.21 = (bf16[256,256]{1,0:T(8,128)(2,1)}, bf16[256,256]{1,0:T(8,128)(2,1)S(1)}, u32[]{:S(2)}, u32[]{:S(2)}) collective-permute-start(bf16[256,256]{1,0:T(8,128)(2,1)} %get-tuple-element.29), channel_id=1, source_target_pairs={{0,64},{8,72},{16,80},{24,88},{32,96},{40,104},{48,112},{56,120},{... | collective-permute-start | bytes 393224 | tf_op jit(solution)/shard_map/ppermute | solution.py:24
  98.3 68.0 %copy-start.2 = (bf16[4,256,128]{2,1,0:T(8,128)(2,1)}, bf16[4,256,128]{2,1,0:T(8,128)(2,1)S(1)}, u32[]{:S(2)}) copy-start(bf16[4,256,128]{2,1,0:T(8,128)(2,1)S(1)} %pad_maximum_fusion.1.a_ref) | copy-start | bytes 786436
  106.8 39.7 %collective-permute-start.16 = (bf16[4,256,128]{2,1,0:T(8,128)(2,1)S(1)}, bf16[4,256,128]{2,1,0:T(8,128)(2,1)S(1)}, u32[]{:S(2)}, u32[]{:S(2)}) collective-permute-start(bf16[4,256,128]{2,1,0:T(8,128)(2,1)S(1)} %pad_maximum_fusion.1.a_ref), channel_id=1, source_target_pairs={{0,16},{8,24},{16,0},{24,8},{32,48},{40,56},{48,32},{56,40},{64,80... | collective-permute-start | bytes 786440 | tf_op jit(solution)/shard_map/ppermute | solution.py:24
  146.5 19.5 %copy-start.5 = (bf16[4,256,128]{2,1,0:T(8,128)(2,1)}, bf16[4,256,128]{2,1,0:T(8,128)(2,1)S(1)}, u32[]{:S(2)}) copy-start(bf16[4,256,128]{2,1,0:T(8,128)(2,1)S(1)} %collective-permute-done.16.b_ref) | copy-start | bytes 786436
  146.5 2.9 %collective-permute-start.17 = (bf16[4,256,128]{2,1,0:T(8,128)(2,1)S(1)}, bf16[4,256,128]{2,1,0:T(8,128)(2,1)S(1)}, u32[]{:S(2)}, u32[]{:S(2)}) collective-permute-start(bf16[4,256,128]{2,1,0:T(8,128)(2,1)S(1)} %pad_maximum_fusion.1.a_ref), channel_id=1, source_target_pairs={{0,8},{8,0},{16,24},{24,16},{32,40},{40,32},{48,56},{56,48},{64,72... | collective-permute-start | bytes 786440 | tf_op jit(solution)/shard_map/ppermute | solution.py:24
  149.3 16.6 %copy-start.6 = (bf16[4,256,128]{2,1,0:T(8,128)(2,1)}, bf16[4,256,128]{2,1,0:T(8,128)(2,1)S(1)}, u32[]{:S(2)}) copy-start(bf16[4,256,128]{2,1,0:T(8,128)(2,1)S(1)} %collective-permute-done.17.c_ref) | copy-start | bytes 786436
  149.3 1.5 collective-permute-start.18
  149.8 25.7 %copy-start.1 = (bf16[4,256,256]{2,1,0:T(8,128)(2,1)}, bf16[4,256,256]{2,1,0:T(8,128)(2,1)S(1)}, u32[]{:S(2)}) copy-start(bf16[4,256,256]{2,1,0:T(8,128)(2,1)S(1)} %pad_maximum_fusion.mine_ref) | copy-start | bytes 1572868
  150.9 15.1 %copy-start.7 = (bf16[4,256,128]{2,1,0:T(8,128)(2,1)}, bf16[4,256,128]{2,1,0:T(8,128)(2,1)S(1)}, u32[]{:S(2)}) copy-start(bf16[4,256,128]{2,1,0:T(8,128)(2,1)S(1)} %collective-permute-done.18.d_ref) | copy-start | bytes 786436
  150.9 14.1 %collective-permute-start.22 = (bf16[4,256,256]{2,1,0:T(8,128)(2,1)S(1)}, bf16[4,256,256]{2,1,0:T(8,128)(2,1)S(1)}, u32[]{:S(2)}, u32[]{:S(2)}) collective-permute-start(bf16[4,256,256]{2,1,0:T(8,128)(2,1)S(1)} %pad_maximum_fusion.mine_ref), channel_id=1, source_target_pairs={{0,16},{8,24},{16,0},{24,8},{32,48},{40,56},{48,32},{56,40},{64,80... | collective-permute-start | bytes 1572872 | tf_op jit(solution)/shard_map/ppermute | solution.py:24
  153.1 48.3 %collective-permute-start.26 = (bf16[4,64,2048]{2,1,0:T(8,128)(2,1)}, bf16[4,64,2048]{2,1,0:T(8,128)(2,1)}, u32[]{:S(2)}, u32[]{:S(2)}) collective-permute-start(bf16[4,64,2048]{2,1,0:T(8,128)(2,1)} %collective-permute-done.25.rest_1_), channel_id=1, source_target_pairs={{0,8},{8,0},{16,24},{24,16},{32,40},{40,32},{48,56},{56,48},{64,72... | collective-permute-start | bytes 3145736 | tf_op jit(solution)/shard_map/ppermute | solution.py:24
  165.0 10.5 %copy-start.4 = (bf16[4,256,256]{2,1,0:T(8,128)(2,1)}, bf16[4,256,256]{2,1,0:T(8,128)(2,1)S(1)}, u32[]{:S(2)}) copy-start(bf16[4,256,256]{2,1,0:T(8,128)(2,1)S(1)} %collective-permute-done.22.mine_ref) | copy-start | bytes 1572868
  165.0 28.2 %collective-permute-start.27 = (bf16[4,256,256]{2,1,0:T(8,128)(2,1)S(1)}, bf16[4,256,256]{2,1,0:T(8,128)(2,1)}, u32[]{:S(2)}, u32[]{:S(2)}) collective-permute-start(bf16[4,256,256]{2,1,0:T(8,128)(2,1)S(1)} %pad_maximum_fusion.mine_ref), channel_id=1, source_target_pairs={{0,8},{8,0},{16,24},{24,16},{32,40},{40,32},{48,56},{56,48},{64,72... | collective-permute-start | bytes 1572872 | tf_op jit(solution)/shard_map/ppermute | solution.py:24
  166.0 9.5 %copy-start = (bf16[272,4096]{1,0:T(8,128)(2,1)}, bf16[272,4096]{1,0:T(8,128)(2,1)S(1)}, u32[]{:S(2)}) copy-start(bf16[272,4096]{1,0:T(8,128)(2,1)S(1)} %collective-permute-done.first_ref) | copy-start | bytes 6684676
  166.0 35.3 %collective-permute-start.23 = (bf16[4,256,256]{2,1,0:T(8,128)(2,1)S(1)}, bf16[4,256,256]{2,1,0:T(8,128)(2,1)}, u32[]{:S(2)}, u32[]{:S(2)}) collective-permute-start(bf16[4,256,256]{2,1,0:T(8,128)(2,1)S(1)} %collective-permute-done.22.mine_ref), channel_id=1, source_target_pairs={{0,8},{8,0},{16,24},{24,16},{32,40},{40,32},{48,56},{56,48},{64,72... | collective-permute-start | bytes 1572872 | tf_op jit(solution)/shard_map/ppermute | solution.py:24
Sparse Core Ops, SparseCore 0:
  9.7 61.7 all-gather.5
  73.1 49.6 all-gather.3
